TPU v7x, 32 devices: a whole 2x2x4 slice. The times are simulated.
32 devices in a mesh: replica: 8 (over z, core), fsdp: 4 (over y, x).
Axes of the slice: x: 2, y: 2, z: 4, core: 2. Of those that a mesh axis runs over, the one named last changes fastest.
Arguments:
- tokens: bfloat16 [2, 2048, 2048], P(None, ('replica', 'fsdp')), may hold values from -6 to 6
- cotangent: bfloat16 [2, 2048, 2048], P(None, ('replica', 'fsdp'))
- parents: int32 [2, 8, 13], P(None, 'replica'), may hold values from 0 to 11, as said below
- lengths: int32 [2, 8, 13], P(None, 'replica'), may hold values from 1 to 128, 256 in all within a row
- qkv_weight: bfloat16 [3, 2048, 2048], P(None, None, 'fsdp')
- out_weight: bfloat16 [2048, 2048], P('fsdp'), may hold values from -0.125 to 0.125
- gate_up_weight: bfloat16 [2, 2048, 8192], P(None, None, 'fsdp'), may hold values from -0.125 to 0.125
- down_weight: bfloat16 [8192, 2048], P('fsdp'), may hold values from -0.0625 to 0.0625
- qk_gain: float32 [2, 2048], P(None, 'fsdp'), may hold values from 1.1 to 1.9
- post_gain: float32 [2, 2048], replicated, may hold values from 0.5 to 1.5
Outputs:
- output: float32 [2, 2048, 2048], P(None, ('replica', 'fsdp'))
- input_grad: float32 [2, 2048, 2048], P(None, ('replica', 'fsdp'))
- qkv_grad: float32 [3, 2048, 2048], P(None, 'replica', 'fsdp')
- out_grad: float32 [2048, 2048], P('fsdp', 'replica')
- gate_up_grad: float32 [2, 2048, 8192], P(None, 'replica', 'fsdp')
- down_grad: float32 [8192, 2048], P('fsdp', 'replica')
- qk_gain_grad: float32 [2, 2048], P(None, 'fsdp')
- post_gain_grad: float32 [2, 2048], P(None, 'fsdp')
Inputs may be any that keep to these rules, and one draw needn't show every extreme that they name: parents[..., 0] = 0 and parents[..., s] < s for every later segment s, so a tree's root is segment 0. The lengths of one tree add up to 256, and the largest is exactly 128.
All inputs are finite; a program needn't handle non-finite values.
Results may differ from a plain program's by a relative error of at most 0.02.
Values may be sent and summed in bfloat16 or wider, within the bound.
No kernel may reach another device: no remote copies, remote signals or barrier semaphores. Data moves between devices by JAX's collectives and lax.ppermute only.
A program may use at most 256 MiB of HBM per device.

v0:
```python
import jax
import jax.numpy as jnp
from jax import lax
from jax.sharding import PartitionSpec as P

HD = 128


EPSILON = 1e-06
ROPE_BASE = 500000.0


def tree_layout(parent_row, length_row, group_rows):
    segments = parent_row.shape[0]
    ends = jnp.cumsum(length_row)
    starts = ends - length_row
    places = jnp.arange(group_rows, dtype=jnp.int32)
    labels = jnp.arange(segments, dtype=jnp.int32)
    segment_of = jnp.sum((places[:, None] >= ends[None, :]).astype(jnp.int32), axis=1)
    member = segment_of[:, None] == labels[None, :]
    walker = labels
    ancestry = walker[:, None] == labels[None, :]
    for depth_step in range(segments - 1):
        walker = jnp.sum(
            jnp.where(walker[:, None] == labels[None, :], parent_row[None, :], 0), axis=1
        )
        ancestry = ancestry | (walker[:, None] == labels[None, :])
    above = jnp.sum(jnp.where(ancestry, length_row[None, :], 0), axis=1) - length_row
    moved = jnp.sum(jnp.where(member, (above - starts)[None, :], 0), axis=1)
    position = (places + moved).astype(jnp.float32)
    member_f = member.astype(jnp.float32)
    reach = jnp.dot(member_f, ancestry.astype(jnp.float32))
    return (member_f, reach, position)


def rope_tables(position, head_dim):
    freq = ROPE_BASE ** (-jnp.arange(0, head_dim, 2, dtype=jnp.float32) / head_dim)
    angle = position[:, None] * freq[None, :]
    angle = jnp.concatenate([angle, angle], axis=1)
    return (jnp.cos(angle)[:, None, :], jnp.sin(angle)[:, None, :])


def rotate(field, cos_t, sin_t):
    half = field.shape[-1] // 2
    turned = jnp.concatenate([-field[..., half:], field[..., :half]], axis=-1)
    return field * cos_t + turned * sin_t


def unrotate(grad_field, cos_t, sin_t):
    half = grad_field.shape[-1] // 2
    sined = grad_field * sin_t
    turned = jnp.concatenate([sined[..., half:], -sined[..., :half]], axis=-1)
    return grad_field * cos_t + turned


def block_visible(reach, member_f, first_row, block_rows, group_rows):
    near = jnp.dot(reach, member_f.T) > 0.5
    row_ids = first_row + jnp.arange(block_rows)[:, None]
    col_ids = jnp.arange(group_rows)[None, :]
    return near & (col_ids <= row_ids)


def block_scores(query_block, lookups, visible, score_scale):
    raw = (
        jnp.einsum("bhd,khd->hbk", query_block, lookups, preferred_element_type=jnp.float32)
        * score_scale
    )
    return jnp.where(visible[None], raw, -1e30)


def norm_back(field, inv_rms, gain, upstream, model_width, partner_sum):
    weighted = upstream * gain
    return inv_rms[:, None] * weighted - field * (inv_rms**3 * partner_sum / model_width)[:, None]


def micro_step(
    x_rows,
    grad_rows,
    parent_row,
    length_row,
    qkv_weight,
    out_weight,
    gate_up_weight,
    down_weight,
    qk_gain,
    post_gain,
):
    tok_dev, model_width = x_rows.shape
    group_rows = tok_dev * lax.axis_size("fsdp")
    local_width = qkv_weight.shape[2]
    local_heads = local_width // HD
    block_rows = min(512, group_rows)
    score_scale = HD ** (-0.5)
    member_f, reach, position = tree_layout(parent_row, length_row, group_rows)
    cos_t, sin_t = rope_tables(position, HD)
    shard_rows = lax.all_gather(x_rows, "fsdp", axis=0, tiled=True)
    product = jnp.einsum("td,nde->tne", shard_rows, qkv_weight, preferred_element_type=jnp.float32)
    gathered_x = (shard_rows, product)
    projected = gathered_x[-1]
    query_raw = projected[:, 0]
    key_raw = projected[:, 1]
    squares = lax.psum(
        jnp.stack([jnp.sum(query_raw * query_raw, axis=1), jnp.sum(key_raw * key_raw, axis=1)]),
        "fsdp",
    )
    inv_rms = lax.rsqrt(squares / model_width + EPSILON)
    queries = rotate(
        (query_raw * inv_rms[0][:, None] * qk_gain[0]).reshape(group_rows, local_heads, HD),
        cos_t,
        sin_t,
    ).astype(jnp.bfloat16)
    lookups = rotate(
        (key_raw * inv_rms[1][:, None] * qk_gain[1]).reshape(group_rows, local_heads, HD),
        cos_t,
        sin_t,
    ).astype(jnp.bfloat16)
    contents = projected[:, 2].reshape(group_rows, local_heads, HD).astype(jnp.bfloat16)
    first_row = 0
    visible = block_visible(reach, member_f, first_row, block_rows, group_rows)
    scores = block_scores(queries, lookups, visible, score_scale)
    row_max = jnp.max(scores, axis=2)
    raw_weights = jnp.exp(scores - row_max[:, :, None])
    row_total = jnp.sum(raw_weights, axis=2)
    prob_rows = (raw_weights / row_total[:, :, None]).astype(jnp.bfloat16)
    context_parts = jnp.einsum(
        "hbk,khd->bhd", prob_rows, contents, preferred_element_type=jnp.float32
    ).astype(jnp.bfloat16)
    total_parts = row_max + jnp.log(row_total)
    context = context_parts.reshape(group_rows, local_width)
    attn = lax.psum_scatter(
        jnp.dot(context, out_weight, preferred_element_type=jnp.float32),
        "fsdp",
        scatter_dimension=0,
        tiled=True,
    )
    rms_attn = lax.rsqrt(jnp.mean(attn * attn, axis=1) + EPSILON)
    hidden = x_rows.astype(jnp.float32) + attn * rms_attn[:, None] * post_gain[0]
    hidden_b = hidden.astype(jnp.bfloat16)
    shard_rows = lax.all_gather(hidden_b, "fsdp", axis=0, tiled=True)
    product = jnp.einsum(
        "td,ndf->tnf", shard_rows, gate_up_weight, preferred_element_type=jnp.float32
    )
    gathered_h = (shard_rows, product)
    gate_up = gathered_h[-1]
    gate_pre = gate_up[:, 0]
    up_pre = gate_up[:, 1]
    sigmoid_gate = jax.nn.sigmoid(gate_pre)
    silu_gate = gate_pre * sigmoid_gate
    swiglu = (silu_gate * up_pre).astype(jnp.bfloat16)
    mlp = lax.psum_scatter(
        jnp.dot(swiglu, down_weight, preferred_element_type=jnp.float32),
        "fsdp",
        scatter_dimension=0,
        tiled=True,
    )
    rms_mlp = lax.rsqrt(jnp.mean(mlp * mlp, axis=1) + EPSILON)
    out_rows = hidden + mlp * rms_mlp[:, None] * post_gain[1]
    upstream = grad_rows.astype(jnp.float32)
    gain_mlp = jnp.sum(upstream * mlp * rms_mlp[:, None], axis=0)
    d_mlp = norm_back(
        mlp,
        rms_mlp,
        post_gain[1],
        upstream,
        model_width,
        jnp.sum(mlp * post_gain[1] * upstream, axis=1),
    ).astype(jnp.bfloat16)
    shard_rows = lax.all_gather(d_mlp, "fsdp", axis=0, tiled=True)
    d_mlp_full = shard_rows
    d_swiglu = jnp.einsum("td,fd->tf", shard_rows, down_weight, preferred_element_type=jnp.float32)
    grad_down = jnp.einsum("tf,td->fd", swiglu, d_mlp_full, preferred_element_type=jnp.float32)
    d_gate = d_swiglu * up_pre * sigmoid_gate * (1.0 + gate_pre * (1.0 - sigmoid_gate))
    d_up = d_swiglu * silu_gate
    d_gate_up = jnp.stack([d_gate, d_up], axis=1).astype(jnp.bfloat16)
    grad_gate_up = jnp.einsum(
        "td,tnf->ndf", gathered_h[0], d_gate_up, preferred_element_type=jnp.float32
    )
    part_rows = d_gate_up
    d_hidden = upstream + lax.psum_scatter(
        jnp.einsum("tnf,ndf->td", part_rows, gate_up_weight, preferred_element_type=jnp.float32),
        "fsdp",
        scatter_dimension=0,
        tiled=True,
    )
    gain_attn = jnp.sum(d_hidden * attn * rms_attn[:, None], axis=0)
    d_attn = norm_back(
        attn,
        rms_attn,
        post_gain[0],
        d_hidden,
        model_width,
        jnp.sum(attn * post_gain[0] * d_hidden, axis=1),
    ).astype(jnp.bfloat16)
    shard_rows = lax.all_gather(d_attn, "fsdp", axis=0, tiled=True)
    d_context = jnp.einsum("td,cd->tc", shard_rows, out_weight, preferred_element_type=jnp.float32)
    grad_out = jnp.einsum("tc,td->cd", context, shard_rows, preferred_element_type=jnp.float32)
    d_context_b = d_context.astype(jnp.bfloat16).reshape(group_rows, local_heads, HD)
    first_row = 0
    visible = block_visible(reach, member_f, first_row, block_rows, group_rows)
    scores = block_scores(queries, lookups, visible, score_scale)
    prob_f = jnp.exp(scores - total_parts[:, first_row : first_row + block_rows, None])
    prob_rows = prob_f.astype(jnp.bfloat16)
    d_prob = jnp.einsum("bhd,khd->hbk", d_context_b, contents, preferred_element_type=jnp.float32)
    row_delta = jnp.sum(d_prob * prob_f, axis=2)
    d_scores = (prob_f * (d_prob - row_delta[:, :, None])).astype(jnp.bfloat16)
    query_grads = (
        jnp.einsum("hbk,khd->bhd", d_scores, lookups, preferred_element_type=jnp.float32)
        * score_scale
    )
    key_grad = (
        jnp.einsum("hbk,bhd->khd", d_scores, queries, preferred_element_type=jnp.float32)
        * score_scale
    )
    value_grad = jnp.einsum(
        "hbk,bhd->khd", prob_rows, d_context_b, preferred_element_type=jnp.float32
    )
    query_norm_grad = unrotate(query_grads, cos_t, sin_t).reshape(group_rows, local_width)
    key_norm_grad = unrotate(key_grad, cos_t, sin_t).reshape(group_rows, local_width)
    gain_query = jnp.sum(query_norm_grad * query_raw * inv_rms[0][:, None], axis=0)
    gain_key = jnp.sum(key_norm_grad * key_raw * inv_rms[1][:, None], axis=0)
    feature_sums = lax.psum(
        jnp.stack(
            [
                jnp.sum(query_raw * qk_gain[0] * query_norm_grad, axis=1),
                jnp.sum(key_raw * qk_gain[1] * key_norm_grad, axis=1),
            ]
        ),
        "fsdp",
    )
    d_query_raw = norm_back(
        query_raw, inv_rms[0], qk_gain[0], query_norm_grad, model_width, feature_sums[0]
    )
    d_key_raw = norm_back(
        key_raw, inv_rms[1], qk_gain[1], key_norm_grad, model_width, feature_sums[1]
    )
    d_projected = jnp.stack(
        [d_query_raw, d_key_raw, value_grad.reshape(group_rows, local_width)], axis=1
    ).astype(jnp.bfloat16)
    grad_qkv = jnp.einsum(
        "td,tne->nde", gathered_x[0], d_projected, preferred_element_type=jnp.float32
    )
    part_rows = d_projected
    input_rows = d_hidden + lax.psum_scatter(
        jnp.einsum("tne,nde->td", part_rows, qkv_weight, preferred_element_type=jnp.float32).astype(
            jnp.bfloat16
        ),
        "fsdp",
        scatter_dimension=0,
        tiled=True,
    ).astype(jnp.float32)
    gain_rows = jnp.stack([gain_attn, gain_mlp])
    query_key_rows = jnp.stack([gain_query, gain_key])
    return (
        out_rows,
        input_rows,
        (grad_qkv, grad_out, grad_gate_up, grad_down),
        gain_rows,
        query_key_rows,
    )


def to_owners(grads):
    return (
        lax.psum_scatter(
            grads[0].astype(jnp.bfloat16), "replica", scatter_dimension=1, tiled=True
        ).astype(jnp.float32),
        lax.psum_scatter(
            grads[1].astype(jnp.bfloat16), "replica", scatter_dimension=1, tiled=True
        ).astype(jnp.float32),
        lax.psum_scatter(
            grads[2].astype(jnp.bfloat16), "replica", scatter_dimension=1, tiled=True
        ).astype(jnp.float32),
        lax.psum_scatter(
            grads[3].astype(jnp.bfloat16), "replica", scatter_dimension=1, tiled=True
        ).astype(jnp.float32),
    )


def on_device(
    tokens,
    cotangent,
    parents,
    lengths,
    qkv_weight,
    out_weight,
    gate_up_weight,
    down_weight,
    qk_gain,
    post_gain,
):
    micro, tok_dev, model_width = tokens.shape
    local_width = qkv_weight.shape[2]
    ff_local = down_weight.shape[0]
    share_rows = model_width // lax.axis_size("replica")
    shares = (
        jnp.zeros((3, share_rows, local_width), jnp.float32),
        jnp.zeros((local_width, share_rows), jnp.float32),
        jnp.zeros((2, share_rows, ff_local), jnp.float32),
        jnp.zeros((ff_local, share_rows), jnp.float32),
    )
    totals = (
        jnp.zeros(qkv_weight.shape, jnp.float32),
        jnp.zeros(out_weight.shape, jnp.float32),
        jnp.zeros(gate_up_weight.shape, jnp.float32),
        jnp.zeros(down_weight.shape, jnp.float32),
    )
    gain_rows = jnp.zeros((2, model_width), jnp.float32)
    query_key_rows = jnp.zeros((2, local_width), jnp.float32)
    outputs = []
    input_grads = []
    for micro_idx in range(micro):
        out_rows, input_rows, grads, gain_add, query_key_add = micro_step(
            tokens[micro_idx],
            cotangent[micro_idx],
            parents[micro_idx, 0],
            lengths[micro_idx, 0],
            qkv_weight,
            out_weight,
            gate_up_weight,
            down_weight,
            qk_gain,
            post_gain,
        )
        outputs.append(out_rows)
        input_grads.append(input_rows)
        gain_rows = gain_rows + gain_add
        query_key_rows = query_key_rows + query_key_add
        totals = tuple((held + added for held, added in zip(totals, grads)))
    shares = to_owners(totals)
    slot = lax.axis_index("fsdp") * local_width
    spread_rows = lax.dynamic_update_slice(
        jnp.zeros((2, model_width), jnp.float32), query_key_rows, (0, slot)
    )
    gain_sum, query_key_sum = lax.psum((gain_rows, spread_rows), ("replica", "fsdp"))
    qk_gain_grad = lax.dynamic_slice(query_key_sum, (0, slot), (2, local_width))
    post_gain_grad = lax.dynamic_slice(gain_sum, (0, slot), (2, local_width))
    return (
        jnp.stack(outputs),
        jnp.stack(input_grads),
        shares[0],
        shares[1],
        shares[2],
        shares[3],
        qk_gain_grad,
        post_gain_grad,
    )


def solution(mesh):
    in_specs = (
        P(None, ("replica", "fsdp"), None),
        P(None, ("replica", "fsdp"), None),
        P(None, "replica", None),
        P(None, "replica", None),
        P(None, None, "fsdp"),
        P("fsdp", None),
        P(None, None, "fsdp"),
        P("fsdp", None),
        P(None, "fsdp"),
        P(),
    )
    out_specs = (
        P(None, ("replica", "fsdp"), None),
        P(None, ("replica", "fsdp"), None),
        P(None, "replica", "fsdp"),
        P("fsdp", "replica"),
        P(None, "replica", "fsdp"),
        P("fsdp", "replica"),
        P(None, "fsdp"),
        P(None, "fsdp"),
    )
    return jax.shard_map(
        on_device, mesh=mesh, in_specs=in_specs, out_specs=out_specs, check_vma=False
    )
```

profile of v0, /device:TPU:0, one launch (start us, length us, event | category | flops | bytes accessed | tf_op | source)
XLA Modules:
  0.0 991.1 jit_solution(8925868820527075536)
XLA Ops:
  21.3 18.4 %all-gather.23.cloned.1.call-done = bf16[1,256,2048]{2,1,0:T(8,128)(2,1)} async-done(((bf16[1,64,2048]{2,1,0:T(8,128)(2,1)}), bf16[1,256,2048]{2,1,0:T(8,128)(2,1)}) %all-gather.23.cloned.1.call-update) | async-done | bytes 1048592 | tf_op jit(solution)/shard_map/all_gather | solution.py:96
  47.3 21.4 %all-gather.25.cloned.1.call-done = bf16[1,256,2048]{2,1,0:T(8,128)(2,1)} async-done(((bf16[1,64,2048]{2,1,0:T(8,128)(2,1)}), bf16[1,256,2048]{2,1,0:T(8,128)(2,1)}) %all-gather.25.cloned.1.call-update) | async-done | bytes 1048592 | tf_op jit(solution)/shard_map/all_gather | solution.py:96
  114.5 21.7 %reduce-scatter.13.cloned.1.call-done = f32[64,2048]{1,0:T(8,128)} async-done(((f32[256,2048]{1,0:T(8,128)}), f32[64,2048]{1,0:T(8,128)}) %reduce-scatter.13.cloned.1.call-update) | async-done | bytes 524304 | tf_op jit(solution)/shard_map/reduce_scatter | solution.py:130
  137.4 37.4 %reduce-scatter.17.cloned.1.call-done = f32[64,2048]{1,0:T(8,128)} async-done(((f32[256,2048]{1,0:T(8,128)}), f32[64,2048]{1,0:T(8,128)}) %reduce-scatter.17.cloned.1.call-update) | async-done | bytes 524304 | tf_op jit(solution)/shard_map/reduce_scatter | solution.py:130
  179.2 25.8 %all-gather.13.cloned.1.call-done = bf16[256,2048]{1,0:T(8,128)(2,1)} async-done(((bf16[64,2048]{1,0:T(8,128)(2,1)}), bf16[256,2048]{1,0:T(8,128)(2,1)}) %all-gather.13.cloned.1.call-update) | async-done | bytes 1048592 | tf_op jit(solution)/shard_map/all_gather | solution.py:139
  223.6 10.2 %all-gather.11.cloned.1.call-done = bf16[256,2048]{1,0:T(8,128)(2,1)} async-done(((bf16[64,2048]{1,0:T(8,128)(2,1)}), bf16[256,2048]{1,0:T(8,128)(2,1)}) %all-gather.11.cloned.1.call-update) | async-done | bytes 1048592 | tf_op jit(solution)/shard_map/all_gather | solution.py:139
  252.4 19.6 %reduce-scatter.19.cloned.1.call-done = f32[64,2048]{1,0:T(8,128)} async-done(((f32[256,2048]{1,0:T(8,128)}), f32[64,2048]{1,0:T(8,128)}) %reduce-scatter.19.cloned.1.call-update) | async-done | bytes 524304 | tf_op jit(solution)/shard_map/reduce_scatter | solution.py:150
  273.3 37.6 %reduce-scatter.15.cloned.1.call-done = f32[64,2048]{1,0:T(8,128)} async-done(((f32[256,2048]{1,0:T(8,128)}), f32[64,2048]{1,0:T(8,128)}) %reduce-scatter.15.cloned.1.call-update) | async-done | bytes 524304 | tf_op jit(solution)/shard_map/reduce_scatter | solution.py:150
  316.4 25.8 %all-gather.15.cloned.1.call-done = bf16[256,2048]{1,0:T(8,128)(2,1)} async-done(((bf16[64,2048]{1,0:T(8,128)(2,1)}), bf16[256,2048]{1,0:T(8,128)(2,1)}) %all-gather.15.cloned.1.call-update) | async-done | bytes 1048592 | tf_op jit(solution)/shard_map/all_gather | solution.py:168
  342.1 9.1 fusion.34
  351.2 12.4 %convolution_bitcast_fusion.3 = f32[256,2048]{1,0:T(8,128)} fusion(bf16[2,2048,2048]{2,1,0:T(8,128)(2,1)} %param.16, bf16[256,1,2048]{2,0,1:T(8,128)(2,1)} %get-tuple-element.65, bf16[256,1,2048]{2,0,1:T(8,128)(2,1)} %get-tuple-element.64), kind=kOutput, calls=%fused_computation.9 | convolution fusion | flops 4296015872 | bytes 20971520 | tf_op jit(solution)/shard_map/tnf,ndf->td/dot_general | solution.py:180
  380.0 12.5 %convolution_bitcast_fusion.2 = f32[256,2048]{1,0:T(8,128)} fusion(bf16[2,2048,2048]{2,1,0:T(8,128)(2,1)} %param.16, bf16[256,1,2048]{2,0,1:T(8,128)(2,1)} %get-tuple-element.63, bf16[256,1,2048]{2,0,1:T(8,128)(2,1)} %get-tuple-element.62), kind=kOutput, calls=%fused_computation.8 | convolution fusion | flops 4296015872 | bytes 20971520 | tf_op jit(solution)/shard_map/tnf,ndf->td/dot_general | solution.py:180
  392.5 16.6 %reduce-scatter.21.cloned.1.call-done = f32[64,2048]{1,0:T(8,128)} async-done(((f32[256,2048]{1,0:T(8,128)}), f32[64,2048]{1,0:T(8,128)}) %reduce-scatter.21.cloned.1.call-update) | async-done | bytes 524304 | tf_op jit(solution)/shard_map/reduce_scatter | solution.py:179
  409.1 38.6 %reduce-scatter.25.cloned.1.call-done = f32[64,2048]{1,0:T(8,128)} async-done(((f32[256,2048]{1,0:T(8,128)}), f32[64,2048]{1,0:T(8,128)}) %reduce-scatter.25.cloned.1.call-update) | async-done | bytes 524304 | tf_op jit(solution)/shard_map/reduce_scatter | solution.py:179
  454.2 25.8 %all-gather.21.cloned.1.call-done = bf16[256,2048]{1,0:T(8,128)(2,1)} async-done(((bf16[64,2048]{1,0:T(8,128)(2,1)}), bf16[256,2048]{1,0:T(8,128)(2,1)}) %all-gather.21.cloned.1.call-update) | async-done | bytes 1048592 | tf_op jit(solution)/shard_map/all_gather | solution.py:194
  491.0 17.8 %all-gather.17.cloned.1.call-done = bf16[256,2048]{1,0:T(8,128)(2,1)} async-done(((bf16[64,2048]{1,0:T(8,128)(2,1)}), bf16[256,2048]{1,0:T(8,128)(2,1)}) %all-gather.17.cloned.1.call-update) | async-done | bytes 1048592 | tf_op jit(solution)/shard_map/all_gather | solution.py:194
  527.2 9.1 all-reduce.1
  571.5 11.6 %add_convert_fusion.1 = bf16[2048,2048]{1,0:T(8,128)(2,1)} fusion(f32[2048,2048]{1,0:T(8,128)} %fusion.149, bf16[256,2048]{1,0:T(8,128)(2,1)S(1)} %copy-done.31, bf16[256,2048]{1,0:T(8,128)(2,1)S(1)} %copy-done.66), kind=kOutput, calls=%fused_computation.2 | convolution fusion | flops 2155872256 | bytes 27262976 | tf_op jit(solution)/shard_map/tf,td->fd/dot_general | solution.py:171
  592.5 14.7 %fusion.8 = f32[2,2048,2048]{2,1,0:T(8,128)} fusion(bf16[256,1,2048]{2,0,1:T(8,128)(2,1)} %get-tuple-element.65, bf16[256,1,2048]{2,0,1:T(8,128)(2,1)S(1)} %copy-done.48, bf16[256,2048]{1,0:T(8,128)(2,1)S(1)} %copy-done.26), kind=kOutput, calls=%fused_computation.32 | convolution fusion | flops 4296015872 | bytes 36700160 | tf_op jit(solution)/shard_map/td,tnf->ndf/dot_general | solution.py:175
  607.2 17.1 %fusion = bf16[2,2048,2048]{1,2,0:T(8,128)(2,1)} fusion(f32[2,2048,2048]{2,1,0:T(8,128)} %fusion.8, bf16[256,1,2048]{2,0,1:T(8,128)(2,1)S(1)} %copy-done.70, bf16[256,1,2048]{2,0,1:T(8,128)(2,1)S(1)} %copy-done.69, bf16[256,2048]{1,0:T(8,128)(2,1)S(1)} %copy-done.32), kind=kOutput, calls=%fused_computation.1 | convolution fusion | flops 4312793088 | bytes 53477376 | tf_op jit(solution)/shard_map/td,tnf->ndf/dot_general | solution.py:175
  626.7 39.8 %all-reduce = (f32[2,2048]{1,0:T(2,128)S(1)}, f32[2,2048]{1,0:T(2,128)S(1)}) all-reduce(f32[2,2048]{1,0:T(2,128)S(1)} %fusion.104, f32[2,2048]{1,0:T(2,128)S(1)} %maximum_add_fusion.4), channel_id=1, replica_groups=mesh['replica'=8,'fsdp'=4] {'replica','fsdp'}, use_global_device_ids=true, to_apply=%region_74.75 | all-reduce | flops 8192 | bytes 65536 | tf_op jit(solution)/shard_map/psum | solution.py:334
  671.8 68.5 %reduce-scatter.35.cloned.1.call-done = bf16[2048,256]{1,0:T(8,128)(2,1)} async-done(((bf16[2048,2048]{1,0:T(8,128)(2,1)}), bf16[2048,256]{1,0:T(8,128)(2,1)}) %reduce-scatter.35.cloned.1.call-update) | async-done | bytes 1048592 | tf_op jit(solution)/shard_map/reduce_scatter | solution.py:273
  743.1 67.8 %reduce-scatter.29.cloned.1.call-done = bf16[3,256,512]{1,2,0:T(8,128)(2,1)} async-done(((bf16[3,2048,512]{1,2,0:T(8,128)(2,1)}), bf16[3,256,512]{1,2,0:T(8,128)(2,1)}) %reduce-scatter.29.cloned.1.call-update) | async-done | bytes 786448 | tf_op jit(solution)/shard_map/reduce_scatter | solution.py:264
  813.6 166.2 %reduce-scatter.33.cloned.1.call-done = bf16[2,256,2048]{1,2,0:T(8,128)(2,1)} async-done(((bf16[2,2048,2048]{1,2,0:T(8,128)(2,1)}), bf16[2,256,2048]{1,2,0:T(8,128)(2,1)}) %reduce-scatter.33.cloned.1.call-update) | async-done | bytes 2097168 | tf_op jit(solution)/shard_map/reduce_scatter | solution.py:270
  (429 shorter events, 229.5 us)
Async XLA Ops:
  7.2 91.6 %copy-start = (bf16[512,2048]{1,0:T(8,128)(2,1)S(1)}, bf16[512,2048]{1,0:T(8,128)(2,1)}, u32[]{:S(2)}) copy-start(bf16[512,2048]{1,0:T(8,128)(2,1)} %param.15) | copy-start | bytes 6291460
  7.2 32.5 %all-gather.23.cloned.1.call-start = ((), (), s32[]{:S(2)}) async-start(), calls=%async_computation.30 | async-start | bytes 1310720 | tf_op jit(solution)/shard_map/all_gather | solution.py:96
  9.3 59.4 %all-gather.25.cloned.1.call-start = ((), (), s32[]{:S(2)}) async-start(), calls=%async_computation.31 | async-start | bytes 1310720 | tf_op jit(solution)/shard_map/all_gather | solution.py:96
  10.0 126.2 %reduce-scatter.13.cloned.1.call-start = ((), (), s32[]{:S(2)}) async-start(), calls=%async_computation.12 | async-start | bytes 2621440 | tf_op jit(solution)/shard_map/reduce_scatter | solution.py:130
  100.9 73.9 %reduce-scatter.17.cloned.1.call-start = ((), (), s32[]{:S(2)}) async-start(), calls=%async_computation.15 | async-start | bytes 2621440 | tf_op jit(solution)/shard_map/reduce_scatter | solution.py:130
  113.8 91.3 %all-gather.13.cloned.1.call-start = ((), (), s32[]{:S(2)}) async-start(), calls=%async_computation.16 | async-start | bytes 1310720 | tf_op jit(solution)/shard_map/all_gather | solution.py:139
  178.4 55.5 %all-gather.11.cloned.1.call-start = ((), (), s32[]{:S(2)}) async-start(), calls=%async_computation.13 | async-start | bytes 1310720 | tf_op jit(solution)/shard_map/all_gather | solution.py:139
  179.0 93.1 %reduce-scatter.19.cloned.1.call-start = ((), (), s32[]{:S(2)}) async-start(), calls=%async_computation.17 | async-start | bytes 2621440 | tf_op jit(solution)/shard_map/reduce_scatter | solution.py:150
  223.6 87.3 %reduce-scatter.15.cloned.1.call-start = ((), (), s32[]{:S(2)}) async-start(), calls=%async_computation.14 | async-start | bytes 2621440 | tf_op jit(solution)/shard_map/reduce_scatter | solution.py:150
  252.4 89.7 %all-gather.15.cloned.1.call-start = ((), (), s32[]{:S(2)}) async-start(), calls=%async_computation.18 | async-start | bytes 1310720 | tf_op jit(solution)/shard_map/all_gather | solution.py:168
  315.5 55.4 %all-gather.19.cloned.1.call-start = ((), (), s32[]{:S(2)}) async-start(), calls=%async_computation.22 | async-start | bytes 1310720 | tf_op jit(solution)/shard_map/all_gather | solution.py:168
  316.1 93.0 %reduce-scatter.21.cloned.1.call-start = ((), (), s32[]{:S(2)}) async-start(), calls=%async_computation.19 | async-start | bytes 2621440 | tf_op jit(solution)/shard_map/reduce_scatter | solution.py:179
  363.7 84.1 %reduce-scatter.25.cloned.1.call-start = ((), (), s32[]{:S(2)}) async-start(), calls=%async_computation.23 | async-start | bytes 2621440 | tf_op jit(solution)/shard_map/reduce_scatter | solution.py:179
  392.5 87.5 %all-gather.21.cloned.1.call-start = ((), (), s32[]{:S(2)}) async-start(), calls=%async_computation.24 | async-start | bytes 1310720 | tf_op jit(solution)/shard_map/all_gather | solution.py:194
  453.3 55.5 %all-gather.17.cloned.1.call-start = ((), (), s32[]{:S(2)}) async-start(), calls=%async_computation.20 | async-start | bytes 1310720 | tf_op jit(solution)/shard_map/all_gather | solution.py:194
  453.9 213.9 %reduce-scatter.27.cloned.1.call-start = ((), (), s32[]{:S(2)}) async-start(), calls=%async_computation.25 | async-start | bytes 1310720 | tf_op jit(solution)/shard_map/reduce_scatter | solution.py:243
  551.7 116.1 %reduce-scatter.23.cloned.1.call-start = ((), (), s32[]{:S(2)}) async-start(), calls=%async_computation.21 | async-start | bytes 1310720 | tf_op jit(solution)/shard_map/reduce_scatter | solution.py:243
  558.4 111.6 %reduce-scatter.31.cloned.1.call-start = ((), (), s32[]{:S(2)}) async-start(), calls=%async_computation.27 | async-start | bytes 2359296 | tf_op jit(solution)/shard_map/reduce_scatter | solution.py:267
  561.8 178.5 %reduce-scatter.35.cloned.1.call-start = ((), (), s32[]{:S(2)}) async-start(), calls=%async_computation.29 | async-start | bytes 9437184 | tf_op jit(solution)/shard_map/reduce_scatter | solution.py:273
  583.1 227.7 %reduce-scatter.29.cloned.1.call-start = ((), (), s32[]{:S(2)}) async-start(), calls=%async_computation.26 | async-start | bytes 7077888 | tf_op jit(solution)/shard_map/reduce_scatter | solution.py:264
  591.0 388.7 %reduce-scatter.33.cloned.1.call-start = ((), (), s32[]{:S(2)}) async-start(), calls=%async_computation.28 | async-start | bytes 18874368 | tf_op jit(solution)/shard_map/reduce_scatter | solution.py:270
  624.5 43.3 %copy-start.8 = (bf16[2,64,2048]{2,1,0:T(8,128)(2,1)S(1)}, bf16[2,64,2048]{2,1,0:T(8,128)(2,1)}, u32[]{:S(2)}) copy-start(bf16[2,64,2048]{2,1,0:T(8,128)(2,1)} %param.11) | copy-start | bytes 1572868
  624.5 43.3 %copy-start.23 = (f32[64,2048]{1,0:T(8,128)S(1)}, f32[64,2048]{1,0:T(8,128)}, u32[]{:S(2)}) copy-start(f32[64,2048]{1,0:T(8,128)} %reduce-scatter.21.cloned.1.call-done) | copy-start | bytes 1572868
  810.9 173.0 %copy-start.1 = (bf16[512,2048]{1,0:T(8,128)(2,1)S(1)}, bf16[512,2048]{1,0:T(8,128)(2,1)}, u32[]{:S(2)}) copy-start(bf16[512,2048]{1,0:T(8,128)(2,1)} %param.15) | copy-start | bytes 6291460
  (108 other events, 397.1 us)
Sparse Core Ops, SparseCore 0:
  10.4 29.2 all-gather.22
  42.1 26.4 all-gather.24
  101.0 35.1 reduce-scatter.12
  139.6 35.1 reduce-scatter.16
  178.5 26.4 all-gather.12
  207.3 26.4 all-gather.10
  236.8 35.1 reduce-scatter.18
  275.6 35.1 reduce-scatter.14
  315.6 26.4 all-gather.14
  344.4 26.4 all-gather.18
  373.9 35.1 reduce-scatter.20
  412.5 35.1 reduce-scatter.24
  453.4 26.4 all-gather.20
  482.2 26.4 all-gather.16
  551.8 27.9 reduce-scatter.26
  583.1 27.9 reduce-scatter.22
  613.8 36.0 reduce-scatter.30
  652.1 88.1 reduce-scatter.34
  742.6 68.1 reduce-scatter.28
  813.1 166.6 reduce-scatter.32
where the time goes:
time: 1000 us; the launch traced here: 991 us
  waiting for transfers between devices  628 us (63%)
  matrix products  177 us (18%)
  blocking collectives  57.8 us (6%)
  other arithmetic  55.4 us (6%)
  local copies, waits for them, and re-layouts  54.2 us (5%)
  between operations  16.1 us (2%)
    reduce_scatter x1, waiting for transfers between devices, to_owners(): lax.psum_scatter(grads[2].astype(jnp.bfloat16), 'replica', scatter_dimens...  166 us
    reduce_scatter x1, waiting for transfers between devices, to_owners(): lax.psum_scatter(grads[3].astype(jnp.bfloat16), 'replica', scatter_dimens...  68.5 us
    reduce_scatter x1, waiting for transfers between devices, to_owners(): lax.psum_scatter(grads[0].astype(jnp.bfloat16), 'replica', scatter_dimens...  67.8 us
    reduce_scatter x2, waiting for transfers between devices, micro_step(): lax.psum_scatter(jnp.dot(context, out_weight, preferred_element_type=jnp....  59.1 us
    reduce_scatter x2, waiting for transfers between devices, micro_step(): lax.psum_scatter(jnp.dot(swiglu, down_weight, preferred_element_type=jnp....  57.2 us
    reduce_scatter x2, waiting for transfers between devices, micro_step(): lax.psum_scatter(jnp.einsum('tnf,ndf->td', part_rows, gate_up_weight, pre...  55.2 us
    all_gather x2, waiting for transfers between devices, micro_step(): shard_rows = lax.all_gather(d_attn, 'fsdp', axis=0, tiled=True)  43.6 us
    psum x1, blocking collectives, on_device(): lax.psum((gain_rows, spread_rows), ('replica', 'fsdp'))  39.8 us
  transfers between devices with their start and end apart: 20, of which 17 were waited for; matrix products, arithmetic and copies ran while one was open for 20% of the time, Pallas kernels for 0%

commit v1 on v0

v1 whole, which is shorter than its diff:
```python
import jax
import jax.numpy as jnp
from jax import lax
from jax.sharding import PartitionSpec as P

HD = 128


EPSILON = 1e-06
ROPE_BASE = 500000.0


def exchange(value, axis, flip):
    size = lax.axis_size(axis)
    return lax.ppermute(value, axis, [(i, i ^ flip) for i in range(size)])


def gather_rows(rows):
    size = lax.axis_size("fsdp")
    return jnp.concatenate(
        [rows] + [exchange(rows, "fsdp", flip) for flip in range(1, size)], axis=0
    )


def scatter_rows(partial):
    size = lax.axis_size("fsdp")
    blocks = jnp.split(partial, size, axis=0)
    total = blocks[0].astype(jnp.float32)
    for flip in range(1, size):
        total = total + exchange(blocks[flip], "fsdp", flip).astype(jnp.float32)
    return total


def sum_small(value, axis):
    size = lax.axis_size(axis)
    flip = 1
    while flip < size:
        value = value + exchange(value, axis, flip)
        flip *= 2
    return value


def sum_row_values(value):
    size = lax.axis_size("fsdp")
    kinds, rows = value.shape
    total = value
    for flip in range(1, size):
        blocks = exchange(value, "fsdp", flip).reshape(kinds, size, rows // size)
        total = total + jnp.concatenate(
            [blocks[:, block ^ flip] for block in range(size)], axis=1
        )
    return total


def true_rows(tok_dev):
    size = lax.axis_size("fsdp")
    block = jnp.arange(size, dtype=jnp.int32) ^ lax.axis_index("fsdp")
    return (block[:, None] * tok_dev + jnp.arange(tok_dev, dtype=jnp.int32)[None, :]).reshape(-1)


def tree_layout(parent_row, length_row, places):
    segments = parent_row.shape[0]
    labels = jnp.arange(segments, dtype=jnp.int32)
    before = labels[:, None] >= labels[None, :]
    ends = jnp.sum(jnp.where(before, length_row[None, :], 0), axis=1)
    starts = ends - length_row
    segment_of = jnp.sum((places[:, None] >= ends[None, :]).astype(jnp.int32), axis=1)
    member = segment_of[:, None] == labels[None, :]
    reach = ((labels[:, None] == labels[None, :]) | (parent_row[:, None] == labels[None, :])).astype(
        jnp.float32
    )
    steps = 1
    while steps < segments - 1:
        reach = (jnp.dot(reach, reach) > 0.5).astype(jnp.float32)
        steps *= 2
    ancestry = reach > 0.5
    above = jnp.sum(jnp.where(ancestry, length_row[None, :], 0), axis=1) - length_row
    moved = jnp.sum(jnp.where(member, (above - starts)[None, :], 0), axis=1)
    position = (places + moved).astype(jnp.float32)
    member_f = member.astype(jnp.float32)
    near = jnp.dot(jnp.dot(member_f, reach), member_f.T) > 0.5
    visible = near & (places[None, :] <= places[:, None])
    return (visible, position)


def rope_tables(position, head_dim):
    freq = ROPE_BASE ** (-jnp.arange(0, head_dim, 2, dtype=jnp.float32) / head_dim)
    angle = position[:, None] * freq[None, :]
    angle = jnp.concatenate([angle, angle], axis=1)
    return (jnp.cos(angle)[:, None, :], jnp.sin(angle)[:, None, :])


def rotate(field, cos_t, sin_t):
    half = field.shape[-1] // 2
    turned = jnp.concatenate([-field[..., half:], field[..., :half]], axis=-1)
    return field * cos_t + turned * sin_t


def unrotate(grad_field, cos_t, sin_t):
    half = grad_field.shape[-1] // 2
    sined = grad_field * sin_t
    turned = jnp.concatenate([sined[..., half:], -sined[..., :half]], axis=-1)
    return grad_field * cos_t + turned


def block_scores(query_block, lookups, visible, score_scale):
    raw = (
        jnp.einsum("bhd,khd->hbk", query_block, lookups, preferred_element_type=jnp.float32)
        * score_scale
    )
    return jnp.where(visible[None], raw, -1e30)


def norm_back(field, inv_rms, gain, upstream, model_width, partner_sum):
    weighted = upstream * gain
    return inv_rms[:, None] * weighted - field * (inv_rms**3 * partner_sum / model_width)[:, None]


def micro_step(
    x_rows,
    grad_rows,
    parent_row,
    length_row,
    qkv_weight,
    out_weight,
    gate_up_weight,
    down_weight,
    qk_gain,
    post_gain,
):
    tok_dev, model_width = x_rows.shape
    group_rows = tok_dev * lax.axis_size("fsdp")
    local_width = qkv_weight.shape[2]
    local_heads = local_width // HD
    score_scale = HD ** (-0.5)
    x_full = gather_rows(x_rows)
    visible, position = tree_layout(parent_row, length_row, true_rows(tok_dev))
    cos_t, sin_t = rope_tables(position, HD)
    projected = jnp.einsum("td,nde->tne", x_full, qkv_weight, preferred_element_type=jnp.float32)
    query_raw = projected[:, 0]
    key_raw = projected[:, 1]
    squares = sum_row_values(
        jnp.stack([jnp.sum(query_raw * query_raw, axis=1), jnp.sum(key_raw * key_raw, axis=1)])
    )
    inv_rms = lax.rsqrt(squares / model_width + EPSILON)
    queries = rotate(
        (query_raw * inv_rms[0][:, None] * qk_gain[0]).reshape(group_rows, local_heads, HD),
        cos_t,
        sin_t,
    ).astype(jnp.bfloat16)
    lookups = rotate(
        (key_raw * inv_rms[1][:, None] * qk_gain[1]).reshape(group_rows, local_heads, HD),
        cos_t,
        sin_t,
    ).astype(jnp.bfloat16)
    contents = projected[:, 2].reshape(group_rows, local_heads, HD).astype(jnp.bfloat16)
    scores = block_scores(queries, lookups, visible, score_scale)
    row_max = jnp.max(scores, axis=2)
    raw_weights = jnp.exp(scores - row_max[:, :, None])
    row_total = jnp.sum(raw_weights, axis=2)
    prob_rows = (raw_weights / row_total[:, :, None]).astype(jnp.bfloat16)
    context_parts = jnp.einsum(
        "hbk,khd->bhd", prob_rows, contents, preferred_element_type=jnp.float32
    ).astype(jnp.bfloat16)
    total_parts = row_max + jnp.log(row_total)
    context = context_parts.reshape(group_rows, local_width)
    attn = scatter_rows(jnp.dot(context, out_weight, preferred_element_type=jnp.bfloat16))
    rms_attn = lax.rsqrt(jnp.mean(attn * attn, axis=1) + EPSILON)
    hidden = x_rows.astype(jnp.float32) + attn * rms_attn[:, None] * post_gain[0]
    hidden_full = gather_rows(hidden.astype(jnp.bfloat16))
    gate_up = jnp.einsum(
        "td,ndf->tnf", hidden_full, gate_up_weight, preferred_element_type=jnp.float32
    )
    gate_pre = gate_up[:, 0]
    up_pre = gate_up[:, 1]
    sigmoid_gate = jax.nn.sigmoid(gate_pre)
    silu_gate = gate_pre * sigmoid_gate
    swiglu = (silu_gate * up_pre).astype(jnp.bfloat16)
    mlp = scatter_rows(jnp.dot(swiglu, down_weight, preferred_element_type=jnp.bfloat16))
    rms_mlp = lax.rsqrt(jnp.mean(mlp * mlp, axis=1) + EPSILON)
    out_rows = hidden + mlp * rms_mlp[:, None] * post_gain[1]
    upstream = grad_rows.astype(jnp.float32)
    gain_mlp = jnp.sum(upstream * mlp * rms_mlp[:, None], axis=0)
    d_mlp = norm_back(
        mlp,
        rms_mlp,
        post_gain[1],
        upstream,
        model_width,
        jnp.sum(mlp * post_gain[1] * upstream, axis=1),
    ).astype(jnp.bfloat16)
    d_mlp_full = gather_rows(d_mlp)
    d_swiglu = jnp.einsum("td,fd->tf", d_mlp_full, down_weight, preferred_element_type=jnp.float32)
    d_gate = d_swiglu * up_pre * sigmoid_gate * (1.0 + gate_pre * (1.0 - sigmoid_gate))
    d_up = d_swiglu * silu_gate
    d_gate_up = jnp.stack([d_gate, d_up], axis=1).astype(jnp.bfloat16)
    d_hidden = upstream + scatter_rows(
        jnp.einsum("tnf,ndf->td", d_gate_up, gate_up_weight, preferred_element_type=jnp.bfloat16)
    )
    gain_attn = jnp.sum(d_hidden * attn * rms_attn[:, None], axis=0)
    d_attn = norm_back(
        attn,
        rms_attn,
        post_gain[0],
        d_hidden,
        model_width,
        jnp.sum(attn * post_gain[0] * d_hidden, axis=1),
    ).astype(jnp.bfloat16)
    d_attn_full = gather_rows(d_attn)
    d_context = jnp.einsum("td,cd->tc", d_attn_full, out_weight, preferred_element_type=jnp.float32)
    d_context_b = d_context.astype(jnp.bfloat16).reshape(group_rows, local_heads, HD)
    scores = block_scores(queries, lookups, visible, score_scale)
    prob_f = jnp.exp(scores - total_parts[:, :, None])
    prob_rows = prob_f.astype(jnp.bfloat16)
    d_prob = jnp.einsum("bhd,khd->hbk", d_context_b, contents, preferred_element_type=jnp.float32)
    row_delta = jnp.sum(d_prob * prob_f, axis=2)
    d_scores = (prob_f * (d_prob - row_delta[:, :, None])).astype(jnp.bfloat16)
    query_grads = (
        jnp.einsum("hbk,khd->bhd", d_scores, lookups, preferred_element_type=jnp.float32)
        * score_scale
    )
    key_grad = (
        jnp.einsum("hbk,bhd->khd", d_scores, queries, preferred_element_type=jnp.float32)
        * score_scale
    )
    value_grad = jnp.einsum(
        "hbk,bhd->khd", prob_rows, d_context_b, preferred_element_type=jnp.float32
    )
    query_norm_grad = unrotate(query_grads, cos_t, sin_t).reshape(group_rows, local_width)
    key_norm_grad = unrotate(key_grad, cos_t, sin_t).reshape(group_rows, local_width)
    gain_query = jnp.sum(query_norm_grad * query_raw * inv_rms[0][:, None], axis=0)
    gain_key = jnp.sum(key_norm_grad * key_raw * inv_rms[1][:, None], axis=0)
    feature_sums = sum_row_values(
        jnp.stack(
            [
                jnp.sum(query_raw * qk_gain[0] * query_norm_grad, axis=1),
                jnp.sum(key_raw * qk_gain[1] * key_norm_grad, axis=1),
            ]
        )
    )
    d_query_raw = norm_back(
        query_raw, inv_rms[0], qk_gain[0], query_norm_grad, model_width, feature_sums[0]
    )
    d_key_raw = norm_back(
        key_raw, inv_rms[1], qk_gain[1], key_norm_grad, model_width, feature_sums[1]
    )
    d_projected = jnp.stack(
        [d_query_raw, d_key_raw, value_grad.reshape(group_rows, local_width)], axis=1
    ).astype(jnp.bfloat16)
    input_rows = d_hidden + scatter_rows(
        jnp.einsum("tne,nde->td", d_projected, qkv_weight, preferred_element_type=jnp.bfloat16)
    )
    saved = (
        x_full,
        d_projected,
        context,
        d_attn_full,
        hidden_full,
        d_gate_up,
        swiglu,
        d_mlp_full,
    )
    return (
        out_rows,
        input_rows,
        saved,
        jnp.stack([gain_attn, gain_mlp]),
        jnp.stack([gain_query, gain_key]),
    )


def to_owners(grad, dim):
    return lax.psum_scatter(grad, "replica", scatter_dimension=dim, tiled=True).astype(jnp.float32)


def weight_grads(saved):
    merged = [jnp.concatenate(parts, axis=0) for parts in zip(*saved)]
    x_full, d_projected, context, d_attn, hidden, d_gate_up, swiglu, d_mlp = merged
    kind = jnp.bfloat16
    down = to_owners(jnp.einsum("tf,td->fd", swiglu, d_mlp, preferred_element_type=kind), 1)
    gate_up = to_owners(jnp.einsum("td,tnf->ndf", hidden, d_gate_up, preferred_element_type=kind), 1)
    out = to_owners(jnp.einsum("tc,td->cd", context, d_attn, preferred_element_type=kind), 1)
    qkv = to_owners(jnp.einsum("td,tne->nde", x_full, d_projected, preferred_element_type=kind), 1)
    return (qkv, out, gate_up, down)


def on_device(
    tokens,
    cotangent,
    parents,
    lengths,
    qkv_weight,
    out_weight,
    gate_up_weight,
    down_weight,
    qk_gain,
    post_gain,
):
    micro, tok_dev, model_width = tokens.shape
    local_width = qkv_weight.shape[2]
    outputs = []
    input_grads = []
    saved = []
    gains = []
    for micro_idx in range(micro):
        out_rows, input_rows, kept, gain_add, query_key_add = micro_step(
            tokens[micro_idx],
            cotangent[micro_idx],
            parents[micro_idx, 0],
            lengths[micro_idx, 0],
            qkv_weight,
            out_weight,
            gate_up_weight,
            down_weight,
            qk_gain,
            post_gain,
        )
        outputs.append(out_rows)
        input_grads.append(input_rows)
        saved.append(kept)
        gains.append((gain_add, query_key_add))
    grads = weight_grads(saved)
    gain_rows = sum(gain for gain, _ in gains)
    query_key_rows = sum(gain for _, gain in gains)
    size = lax.axis_size("fsdp")
    me = lax.axis_index("fsdp")
    split = gain_rows.reshape(2, size, local_width)
    post_rows = lax.dynamic_index_in_dim(split, me, 1, keepdims=False)
    for flip in range(1, size):
        sent = lax.dynamic_index_in_dim(split, me ^ flip, 1, keepdims=False)
        post_rows = post_rows + exchange(sent, "fsdp", flip)
    sums = sum_small(jnp.concatenate([query_key_rows, post_rows], axis=0), "replica")
    return (
        jnp.stack(outputs),
        jnp.stack(input_grads),
        grads[0],
        grads[1],
        grads[2],
        grads[3],
        sums[:2],
        sums[2:],
    )


def solution(mesh):
    in_specs = (
        P(None, ("replica", "fsdp"), None),
        P(None, ("replica", "fsdp"), None),
        P(None, "replica", None),
        P(None, "replica", None),
        P(None, None, "fsdp"),
        P("fsdp", None),
        P(None, None, "fsdp"),
        P("fsdp", None),
        P(None, "fsdp"),
        P(),
    )
    out_specs = (
        P(None, ("replica", "fsdp"), None),
        P(None, ("replica", "fsdp"), None),
        P(None, "replica", "fsdp"),
        P("fsdp", "replica"),
        P(None, "replica", "fsdp"),
        P("fsdp", "replica"),
        P(None, "fsdp"),
        P(None, "fsdp"),
    )
    return jax.shard_map(
        on_device, mesh=mesh, in_specs=in_specs, out_specs=out_specs, check_vma=False
    )
```

time: 1000 us -> 696 us (0.70)
  waiting for transfers between devices: 628 us -> 345 us
  starting transfers between devices: 2.38 us -> 82.5 us
  blocking collectives: 57.8 us -> 0 us
  matrix products: 177 us -> 127 us
  local copies, waits for them, and re-layouts: 54.2 us -> 77.3 us
  other arithmetic: 55.4 us -> 37.8 us
    reduce_scatter x12 -> x4, waiting for transfers between devices: 474 us -> 261 us  [to_owners(): lax.psum_scatter(grad, 'replica', scatter_dimension=dim, tiled=True)]
    all_gather x8 -> x0, waiting for transfers between devices: 152 us -> none  [the longest x2 43.6 us: micro_step(): shard_rows = lax.all_gather(d_attn, 'fsdp', axis=0, tiled=True)]
    ppermute x0 -> x66, waiting for transfers between devices: none -> 83.9 us  [exchange(): return lax.ppermute(value, axis, [(i, i ^ flip) for i in range(size)])]
    ppermute x0 -> x66, starting transfers between devices: none -> 82.1 us  [exchange(): return lax.ppermute(value, axis, [(i, i ^ flip) for i in range(size)])]
    psum x3 -> x0, blocking collectives: 57.8 us -> none  [the longest x1 39.8 us: on_device(): lax.psum((gain_rows, spread_rows), ('replica', 'fsdp'))]
    dot_general x26, matrix products: 166 us -> 120 us  [the longest x2 23.8 us: micro_step(): jnp.einsum('tnf,ndf->td', d_gate_up, gate_up_weight, preferred_element_ty...]
    unnamed x226 -> x312, local copies, waits for them, and re-layouts: 25.9 us -> 33.6 us
  transfers between devices with their start and end apart: 20 -> 70, of which waited for: 17 -> 29; matrix products, arithmetic and copies ran while one was open for 20% -> 28% of each run, Pallas kernels for 0% -> 0%
where the time goes in v1:
time: 696 us; the launch traced here: 686 us
  waiting for transfers between devices  345 us (50%)
  matrix products  127 us (18%)
  starting transfers between devices  82.5 us (12%)
  local copies, waits for them, and re-layouts  77.3 us (11%)
  other arithmetic  37.8 us (5%)
  between operations  16.4 us (2%)
    reduce_scatter x4, waiting for transfers between devices, to_owners(): lax.psum_scatter(grad, 'replica', scatter_dimension=dim, tiled=True)  261 us
    ppermute x66, waiting for transfers between devices, exchange(): return lax.ppermute(value, axis, [(i, i ^ flip) for i in range(size)])  83.9 us
    ppermute x66, starting transfers between devices, exchange(): return lax.ppermute(value, axis, [(i, i ^ flip) for i in range(size)])  82.1 us
    unnamed x312, local copies, waits for them, and re-layouts  33.6 us
    dot_general x2, matrix products, micro_step(): jnp.einsum('tnf,ndf->td', d_gate_up, gate_up_weight, preferred_element_ty...  23.8 us
    dot_general x2, matrix products, micro_step(): jnp.einsum('td,fd->tf', d_mlp_full, down_weight, preferred_element_type=j...  16.9 us
    dot_general x2, matrix products, micro_step(): jnp.einsum('td,ndf->tnf', hidden_full, gate_up_weight, preferred_element_...  16.4 us
    dot_general x1, matrix products, weight_grads(): jnp.einsum('td,tnf->ndf', hidden, d_gate_up, preferred_element_type=kind)  14.7 us
  transfers between devices with their start and end apart: 70, of which 29 were waited for; matrix products, arithmetic and copies ran while one was open for 28% of the time, Pallas kernels for 0%

profile of v1, /device:TPU:0, one launch (start us, length us, event | category | flops | bytes accessed | tf_op | source)
XLA Modules:
  0.0 685.8 jit_solution(2653158234754079224)
XLA Ops:
  28.1 8.4 %collective-permute-done.1 = bf16[64,2048]{1,0:T(8,128)(2,1)S(1)} collective-permute-done((bf16[64,2048]{1,0:T(8,128)(2,1)S(1)}, bf16[64,2048]{1,0:T(8,128)(2,1)S(1)}, u32[]{:S(2)}, u32[]{:S(2)}) %collective-permute-start.1) | collective-permute-done | bytes 262176 | tf_op jit(solution)/shard_map/ppermute | solution.py:15
  36.4 4.8 fusion.46
  45.8 4.9 fusion.60
  85.9 5.1 collective-permute-done.8
  97.1 5.1 collective-permute-done.23
  102.2 6.8 collective-permute-done.22
  116.1 8.3 %fusion.53 = f32[256,2,2048]{2,0,1:T(8,128)S(1)} fusion(bf16[2,2048,2048]{2,1,0:T(8,128)(2,1)} %param.16, bf16[64,2048]{1,0:T(8,128)(2,1)S(1)} %collective-permute-done.11, bf16[64,2048]{1,0:T(8,128)(2,1)S(1)} %collective-permute-done.10, bf16[64,2048]{1,0:T(8,128)(2,1)S(1)} %collective-permute-done.9, bf16[64,2048]{1,0:T(8,128)(2,1)S(1)} %get-tuple-element.59), kind=kOutput, calls=%fused_computation.89 | convolution fusion | flops 4299161600 | bytes 22020096 | tf_op jit(solution)/shard_map/td,ndf->tnf/dot_general | solution.py:171
  132.5 8.1 %fusion.67 = f32[256,2,2048]{2,0,1:T(8,128)S(1)} fusion(bf16[2,2048,2048]{2,1,0:T(8,128)(2,1)} %param.16, bf16[64,2048]{1,0:T(8,128)(2,1)S(1)} %collective-permute-done.26, bf16[64,2048]{1,0:T(8,128)(2,1)S(1)} %collective-permute-done.25, bf16[64,2048]{1,0:T(8,128)(2,1)S(1)} %collective-permute-done.24, bf16[64,2048]{1,0:T(8,128)(2,1)S(1)} %get-tuple-element.57), kind=kOutput, calls=%fused_computation.105 | convolution fusion | flops 4299161600 | bytes 22020096 | tf_op jit(solution)/shard_map/td,ndf->tnf/dot_general | solution.py:171
  166.3 9.5 %collective-permute-done.31 = bf16[64,2048]{1,0:T(8,128)(2,1)S(1)} collective-permute-done((bf16[64,2048]{1,0:T(8,128)(2,1)S(1)}, bf16[64,2048]{1,0:T(8,128)(2,1)S(1)}, u32[]{:S(2)}, u32[]{:S(2)}) %collective-permute-start.31) | collective-permute-done | bytes 262176 | tf_op jit(solution)/shard_map/ppermute | solution.py:15
  181.5 7.7 %fusion.104 = (bf16[256,1,2048]{2,0,1:T(8,128)(2,1)}, bf16[256,1,2048]{2,0,1:T(8,128)(2,1)}) fusion(f32[256,2,2048]{2,0,1:T(8,128)S(1)} %fusion.53, bf16[2048,2048]{1,0:T(8,128)(2,1)S(1)} %bitcast.528, bf16[64,2048]{1,0:T(8,128)(2,1)S(1)} %collective-permute-done.32, bf16[64,2048]{1,0:T(8,128)(2,1)S(1)} %collective-permute-done.31, ...), kind=kOutput, calls=%fused_computation.154 | convolution fusion | flops 2158493696 | bytes 15728640 | tf_op jit(solution)/shard_map/td,fd->tf/dot_general | solution.py:193
  189.3 11.9 %convolution_bitcast_fusion.3 = bf16[256,2048]{1,0:T(8,128)(2,1)} fusion(bf16[2,2048,2048]{2,1,0:T(8,128)(2,1)} %param.16, bf16[256,1,2048]{2,0,1:T(8,128)(2,1)} %get-tuple-element.79, bf16[256,1,2048]{2,0,1:T(8,128)(2,1)} %get-tuple-element.78), kind=kOutput, calls=%fused_computation.10 | convolution fusion | flops 4296015872 | bytes 19922944 | tf_op jit(solution)/shard_map/tnf,ndf->td/dot_general | solution.py:198
  206.8 9.2 %fusion.105 = (bf16[256,1,2048]{2,0,1:T(8,128)(2,1)}, bf16[256,1,2048]{2,0,1:T(8,128)(2,1)}) fusion(f32[256,2,2048]{2,0,1:T(8,128)} %copy-done.22, bf16[2048,2048]{1,0:T(8,128)(2,1)} %param.17, bf16[64,2048]{1,0:T(8,128)(2,1)} %collective-permute-done.47, bf16[64,2048]{1,0:T(8,128)(2,1)} %collective-permute-done.46, ...), kind=kOutput, calls=%fused_computation.155 | convolution fusion | flops 2158493696 | bytes 15728640 | tf_op jit(solution)/shard_map/td,fd->tf/dot_general | solution.py:193
  215.9 11.9 %convolution_bitcast_fusion.2 = bf16[256,2048]{1,0:T(8,128)(2,1)} fusion(bf16[2,2048,2048]{2,1,0:T(8,128)(2,1)} %param.16, bf16[256,1,2048]{2,0,1:T(8,128)(2,1)} %get-tuple-element.81, bf16[256,1,2048]{2,0,1:T(8,128)(2,1)} %get-tuple-element.80), kind=kOutput, calls=%fused_computation.9 | convolution fusion | flops 4296015872 | bytes 19922944 | tf_op jit(solution)/shard_map/tnf,ndf->td/dot_general | solution.py:198
  236.2 5.8 collective-permute-done.50
  299.4 4.3 fusion.142
  324.9 5.4 convolution_bitcast_fusion.1
  335.6 9.9 %fusion.13 = bf16[2048,2048]{1,0:T(8,128)(2,1)} fusion(bf16[512,2048]{1,0:T(8,128)(2,1)} %constant_dynamic-update-slice_fusion.24, bf16[256,2048]{1,0:T(8,128)(2,1)} %copy-done.37, bf16[256,2048]{1,0:T(8,128)(2,1)S(1)} %copy-done.36), kind=kOutput, calls=%fused_computation.23 | convolution fusion | flops 4299161600 | bytes 12582912 | tf_op jit(solution)/shard_map/tf,td->fd/dot_general | solution.py:280
  348.7 14.7 %convolution_bitcast_fusion = bf16[2,2048,2048]{1,2,0:T(8,128)(2,1)} fusion(bf16[256,1,2048]{2,0,1:T(8,128)(2,1)} %get-tuple-element.81, bf16[256,1,2048]{2,0,1:T(8,128)(2,1)} %get-tuple-element.80, bf16[256,1,2048]{2,0,1:T(8,128)(2,1)} %get-tuple-element.79, bf16[256,1,2048]{2,0,1:T(8,128)(2,1)} %get-tuple-element.78, ...), kind=kOutput, calls=%fused_computation | convolution fusion | flops 8606711808 | bytes 23068672 | tf_op jit(solution)/shard_map/td,tnf->ndf/dot_general | solution.py:281
  370.4 4.8 convolution_bitcast_fusion.4
  399.3 5.4 collective-permute-done.44
  409.0 6.7 reduce-scatter.5.cloned.1.call-done
  418.3 87.8 %reduce-scatter.11.cloned.1.call-done = bf16[2048,256]{1,0:T(8,128)(2,1)} async-done(((bf16[2048,2048]{1,0:T(8,128)(2,1)}), bf16[2048,256]{1,0:T(8,128)(2,1)}) %reduce-scatter.11.cloned.1.call-update) | async-done | bytes 1048592 | tf_op jit(solution)/shard_map/reduce_scatter | solution.py:273
  508.8 166.2 %reduce-scatter.9.cloned.1.call-done = bf16[2,256,2048]{1,2,0:T(8,128)(2,1)} async-done(((bf16[2,2048,2048]{1,2,0:T(8,128)(2,1)}), bf16[2,256,2048]{1,2,0:T(8,128)(2,1)}) %reduce-scatter.9.cloned.1.call-update) | async-done | bytes 2097168 | tf_op jit(solution)/shard_map/reduce_scatter | solution.py:273
  674.9 4.1 copy.201
  (618 shorter events, 252.8 us)
Async XLA Ops:
  7.2 400.1 %reduce-scatter.7.cloned.1.call-start = ((), (), s32[]{:S(2)}) async-start(), calls=%async_computation.5 | async-start | bytes 2359296 | tf_op jit(solution)/shard_map/reduce_scatter | solution.py:273
  9.2 36.3 %collective-permute-start.17 = (bf16[64,2048]{1,0:T(8,128)(2,1)}, bf16[64,2048]{1,0:T(8,128)(2,1)}, u32[]{:S(2)}, u32[]{:S(2)}) collective-permute-start(bf16[64,2048]{1,0:T(8,128)(2,1)} %get-tuple-element.137), channel_id=1, source_target_pairs={{0,3},{1,2},{2,1},{3,0},{4,7},{5,6},{6,5},{7,4},{8,11},{9,10},{10,... | collective-permute-start | bytes 786440 | tf_op jit(solution)/shard_map/ppermute | solution.py:15
  13.1 32.7 %collective-permute-start.16 = (bf16[64,2048]{1,0:T(8,128)(2,1)}, bf16[64,2048]{1,0:T(8,128)(2,1)}, u32[]{:S(2)}, u32[]{:S(2)}) collective-permute-start(bf16[64,2048]{1,0:T(8,128)(2,1)} %get-tuple-element.137), channel_id=1, source_target_pairs={{0,2},{1,3},{2,0},{3,1},{4,6},{5,7},{6,4},{7,5},{8,10},{9,11},{10,... | collective-permute-start | bytes 786440 | tf_op jit(solution)/shard_map/ppermute | solution.py:15
  15.1 21.4 %collective-permute-start.1 = (bf16[64,2048]{1,0:T(8,128)(2,1)S(1)}, bf16[64,2048]{1,0:T(8,128)(2,1)S(1)}, u32[]{:S(2)}, u32[]{:S(2)}) collective-permute-start(bf16[64,2048]{1,0:T(8,128)(2,1)S(1)} %get-tuple-element.138), channel_id=1, source_target_pairs={{0,2},{1,3},{2,0},{3,1},{4,6},{5,7},{6,4},{7,5},{8,10},{9,11},{10,... | collective-permute-start | bytes 786440 | tf_op jit(solution)/shard_map/ppermute | solution.py:15
  15.1 21.3 %collective-permute-start = (bf16[64,2048]{1,0:T(8,128)(2,1)S(1)}, bf16[64,2048]{1,0:T(8,128)(2,1)S(1)}, u32[]{:S(2)}, u32[]{:S(2)}) collective-permute-start(bf16[64,2048]{1,0:T(8,128)(2,1)S(1)} %get-tuple-element.138), channel_id=1, source_target_pairs={{0,1},{1,0},{2,3},{3,2},{4,5},{5,4},{6,7},{7,6},{8,9},{9,8},{10,11... | collective-permute-start | bytes 786440 | tf_op jit(solution)/shard_map/ppermute | solution.py:15
  42.3 20.4 %collective-permute-start.4 = (f32[2,256]{1,0:T(2,128)}, f32[2,256]{1,0:T(2,128)}, u32[]{:S(2)}, u32[]{:S(2)}) collective-permute-start(f32[2,256]{1,0:T(2,128)} %pad_maximum_fusion.5), channel_id=1, source_target_pairs={{0,2},{1,3},{2,0},{3,1},{4,6},{5,7},{6,4},{7,5},{8,10},{9,11},{10,... | collective-permute-start | bytes 6152 | tf_op jit(solution)/shard_map/ppermute | solution.py:15
  44.0 19.8 %collective-permute-start.5 = (f32[2,256]{1,0:T(2,128)}, f32[2,256]{1,0:T(2,128)}, u32[]{:S(2)}, u32[]{:S(2)}) collective-permute-start(f32[2,256]{1,0:T(2,128)} %pad_maximum_fusion.5), channel_id=1, source_target_pairs={{0,3},{1,2},{2,1},{3,0},{4,7},{5,6},{6,5},{7,4},{8,11},{9,10},{10,... | collective-permute-start | bytes 6152 | tf_op jit(solution)/shard_map/ppermute | solution.py:15
  45.4 19.2 %collective-permute-start.3 = (f32[2,256]{1,0:T(2,128)}, f32[2,256]{1,0:T(2,128)}, u32[]{:S(2)}, u32[]{:S(2)}) collective-permute-start(f32[2,256]{1,0:T(2,128)} %pad_maximum_fusion.5), channel_id=1, source_target_pairs={{0,1},{1,0},{2,3},{3,2},{4,5},{5,4},{6,7},{7,6},{8,9},{9,8},{10,11... | collective-permute-start | bytes 6152 | tf_op jit(solution)/shard_map/ppermute | solution.py:15
  80.3 21.9 %collective-permute-start.23 = (bf16[64,2048]{1,0:T(8,128)(2,1)S(1)}, bf16[64,2048]{1,0:T(8,128)(2,1)S(1)}, u32[]{:S(2)}, u32[]{:S(2)}) collective-permute-start(bf16[64,2048]{1,0:T(8,128)(2,1)S(1)} %get-tuple-element.109), channel_id=1, source_target_pairs={{0,3},{1,2},{2,1},{3,0},{4,7},{5,6},{6,5},{7,4},{8,11},{9,10},{10,... | collective-permute-start | bytes 786440 | tf_op jit(solution)/shard_map/ppermute | solution.py:15
  84.2 24.8 %collective-permute-start.22 = (bf16[64,2048]{1,0:T(8,128)(2,1)S(1)}, bf16[64,2048]{1,0:T(8,128)(2,1)S(1)}, u32[]{:S(2)}, u32[]{:S(2)}) collective-permute-start(bf16[64,2048]{1,0:T(8,128)(2,1)S(1)} %get-tuple-element.110), channel_id=1, source_target_pairs={{0,2},{1,3},{2,0},{3,1},{4,6},{5,7},{6,4},{7,5},{8,10},{9,11},{10,... | collective-permute-start | bytes 786440 | tf_op jit(solution)/shard_map/ppermute | solution.py:15
  93.4 18.8 %collective-permute-start.11 = (bf16[64,2048]{1,0:T(8,128)(2,1)S(1)}, bf16[64,2048]{1,0:T(8,128)(2,1)S(1)}, u32[]{:S(2)}, u32[]{:S(2)}) collective-permute-start(bf16[64,2048]{1,0:T(8,128)(2,1)S(1)} %get-tuple-element.59), channel_id=1, source_target_pairs={{0,3},{1,2},{2,1},{3,0},{4,7},{5,6},{6,5},{7,4},{8,11},{9,10},{10,... | collective-permute-start | bytes 786440 | tf_op jit(solution)/shard_map/ppermute | solution.py:15
  127.6 19.5 %collective-permute-start.12 = (bf16[64,2048]{1,0:T(8,128)(2,1)S(1)}, bf16[64,2048]{1,0:T(8,128)(2,1)S(1)}, u32[]{:S(2)}, u32[]{:S(2)}) collective-permute-start(bf16[64,2048]{1,0:T(8,128)(2,1)S(1)} %get-tuple-element.102), channel_id=1, source_target_pairs={{0,1},{1,0},{2,3},{3,2},{4,5},{5,4},{6,7},{7,6},{8,9},{9,8},{10,11... | collective-permute-start | bytes 786440 | tf_op jit(solution)/shard_map/ppermute | solution.py:15
  128.0 20.7 %collective-permute-start.14 = (bf16[64,2048]{1,0:T(8,128)(2,1)S(1)}, bf16[64,2048]{1,0:T(8,128)(2,1)S(1)}, u32[]{:S(2)}, u32[]{:S(2)}) collective-permute-start(bf16[64,2048]{1,0:T(8,128)(2,1)S(1)} %get-tuple-element.103), channel_id=1, source_target_pairs={{0,3},{1,2},{2,1},{3,0},{4,7},{5,6},{6,5},{7,4},{8,11},{9,10},{10,... | collective-permute-start | bytes 786440 | tf_op jit(solution)/shard_map/ppermute | solution.py:15
  129.5 19.3 %collective-permute-start.13 = (bf16[64,2048]{1,0:T(8,128)(2,1)S(1)}, bf16[64,2048]{1,0:T(8,128)(2,1)S(1)}, u32[]{:S(2)}, u32[]{:S(2)}) collective-permute-start(bf16[64,2048]{1,0:T(8,128)(2,1)S(1)} %get-tuple-element.104), channel_id=1, source_target_pairs={{0,2},{1,3},{2,0},{3,1},{4,6},{5,7},{6,4},{7,5},{8,10},{9,11},{10,... | collective-permute-start | bytes 786440 | tf_op jit(solution)/shard_map/ppermute | solution.py:15
  178.1 27.3 %collective-permute-start.47 = (bf16[64,2048]{1,0:T(8,128)(2,1)}, bf16[64,2048]{1,0:T(8,128)(2,1)}, u32[]{:S(2)}, u32[]{:S(2)}) collective-permute-start(bf16[64,2048]{1,0:T(8,128)(2,1)} %get-tuple-element.53), channel_id=1, source_target_pairs={{0,3},{1,2},{2,1},{3,0},{4,7},{5,6},{6,5},{7,4},{8,11},{9,10},{10,... | collective-permute-start | bytes 786440 | tf_op jit(solution)/shard_map/ppermute | solution.py:15
  179.5 27.3 %collective-permute-start.46 = (bf16[64,2048]{1,0:T(8,128)(2,1)}, bf16[64,2048]{1,0:T(8,128)(2,1)}, u32[]{:S(2)}, u32[]{:S(2)}) collective-permute-start(bf16[64,2048]{1,0:T(8,128)(2,1)} %get-tuple-element.53), channel_id=1, source_target_pairs={{0,2},{1,3},{2,0},{3,1},{4,6},{5,7},{6,4},{7,5},{8,10},{9,11},{10,... | collective-permute-start | bytes 786440 | tf_op jit(solution)/shard_map/ppermute | solution.py:15
  180.2 26.6 %collective-permute-start.45 = (bf16[64,2048]{1,0:T(8,128)(2,1)}, bf16[64,2048]{1,0:T(8,128)(2,1)}, u32[]{:S(2)}, u32[]{:S(2)}) collective-permute-start(bf16[64,2048]{1,0:T(8,128)(2,1)} %get-tuple-element.53), channel_id=1, source_target_pairs={{0,1},{1,0},{2,3},{3,2},{4,5},{5,4},{6,7},{7,6},{8,9},{9,8},{10,11... | collective-permute-start | bytes 786440 | tf_op jit(solution)/shard_map/ppermute | solution.py:15
  203.3 28.0 %collective-permute-start.33 = (bf16[64,2048]{1,0:T(8,128)(2,1)}, bf16[64,2048]{1,0:T(8,128)(2,1)}, u32[]{:S(2)}, u32[]{:S(2)}) collective-permute-start(bf16[64,2048]{1,0:T(8,128)(2,1)} %get-tuple-element.96), channel_id=1, source_target_pairs={{0,1},{1,0},{2,3},{3,2},{4,5},{5,4},{6,7},{7,6},{8,9},{9,8},{10,11... | collective-permute-start | bytes 786440 | tf_op jit(solution)/shard_map/ppermute | solution.py:15
  204.0 32.1 %collective-permute-start.35 = (bf16[64,2048]{1,0:T(8,128)(2,1)}, bf16[64,2048]{1,0:T(8,128)(2,1)}, u32[]{:S(2)}, u32[]{:S(2)}) collective-permute-start(bf16[64,2048]{1,0:T(8,128)(2,1)} %get-tuple-element.97), channel_id=1, source_target_pairs={{0,3},{1,2},{2,1},{3,0},{4,7},{5,6},{6,5},{7,4},{8,11},{9,10},{10,... | collective-permute-start | bytes 786440 | tf_op jit(solution)/shard_map/ppermute | solution.py:15
  205.4 30.7 %collective-permute-start.34 = (bf16[64,2048]{1,0:T(8,128)(2,1)}, bf16[64,2048]{1,0:T(8,128)(2,1)}, u32[]{:S(2)}, u32[]{:S(2)}) collective-permute-start(bf16[64,2048]{1,0:T(8,128)(2,1)} %get-tuple-element.98), channel_id=1, source_target_pairs={{0,2},{1,3},{2,0},{3,1},{4,6},{5,7},{6,4},{7,5},{8,10},{9,11},{10,... | collective-permute-start | bytes 786440 | tf_op jit(solution)/shard_map/ppermute | solution.py:15
  277.0 20.8 %collective-permute-start.53 = (bf16[64,2048]{1,0:T(8,128)(2,1)}, bf16[64,2048]{1,0:T(8,128)(2,1)}, u32[]{:S(2)}, u32[]{:S(2)}) collective-permute-start(bf16[64,2048]{1,0:T(8,128)(2,1)} %get-tuple-element.61), channel_id=1, source_target_pairs={{0,3},{1,2},{2,1},{3,0},{4,7},{5,6},{6,5},{7,4},{8,11},{9,10},{10,... | collective-permute-start | bytes 786440 | tf_op jit(solution)/shard_map/ppermute | solution.py:15
  308.3 107.5 %reduce-scatter.5.cloned.1.call-start = ((), (), s32[]{:S(2)}) async-start(), calls=%async_computation.4 | async-start | bytes 7077888 | tf_op jit(solution)/shard_map/reduce_scatter | solution.py:273
  330.3 175.7 %reduce-scatter.11.cloned.1.call-start = ((), (), s32[]{:S(2)}) async-start(), calls=%async_computation.7 | async-start | bytes 9437184 | tf_op jit(solution)/shard_map/reduce_scatter | solution.py:273
  345.6 329.4 %reduce-scatter.9.cloned.1.call-start = ((), (), s32[]{:S(2)}) async-start(), calls=%async_computation.6 | async-start | bytes 18874368 | tf_op jit(solution)/shard_map/reduce_scatter | solution.py:273
  (191 other events, 1556.4 us)
Sparse Core Ops, SparseCore 0:
  308.4 36.3 reduce-scatter.6
  347.0 68.6 reduce-scatter.4
  418.0 87.9 reduce-scatter.10
  508.3 166.6 reduce-scatter.8

commit v2 on v1

--- a/solution.py
+++ b/solution.py
@@ -1,6 +1,8 @@
 import jax
 import jax.numpy as jnp
 from jax import lax
+from jax.experimental import pallas as pl
+from jax.experimental.pallas import tpu as pltpu
 from jax.sharding import PartitionSpec as P
 
 HD = 128
@@ -252,11 +254,11 @@
     )
     saved = (
         x_full,
-        d_projected,
+        d_projected.reshape(group_rows, -1),
         context,
         d_attn_full,
         hidden_full,
-        d_gate_up,
+        d_gate_up.reshape(group_rows, -1),
         swiglu,
         d_mlp_full,
     )
@@ -264,24 +266,172 @@
         out_rows,
         input_rows,
         saved,
+        d_mlp,
         jnp.stack([gain_attn, gain_mlp]),
         jnp.stack([gain_query, gain_key]),
     )
 
 
-def to_owners(grad, dim):
-    return lax.psum_scatter(grad, "replica", scatter_dimension=dim, tiled=True).astype(jnp.float32)
-
-
-def weight_grads(saved):
-    merged = [jnp.concatenate(parts, axis=0) for parts in zip(*saved)]
-    x_full, d_projected, context, d_attn, hidden, d_gate_up, swiglu, d_mlp = merged
-    kind = jnp.bfloat16
-    down = to_owners(jnp.einsum("tf,td->fd", swiglu, d_mlp, preferred_element_type=kind), 1)
-    gate_up = to_owners(jnp.einsum("td,tnf->ndf", hidden, d_gate_up, preferred_element_type=kind), 1)
-    out = to_owners(jnp.einsum("tc,td->cd", context, d_attn, preferred_element_type=kind), 1)
-    qkv = to_owners(jnp.einsum("td,tne->nde", x_full, d_projected, preferred_element_type=kind), 1)
-    return (qkv, out, gate_up, down)
+def grad_blocks(order, lefts, rights, width, adds, kind):
+    blocks = order.shape[0]
+    sets = len(lefts)
+    rows = [left.shape[0] for left in lefts]
+    block = lefts[0].shape[1] // lax.axis_size("replica")
+    tile = min(512, width)
+
+    def kernel(order_ref, *refs):
+        left_refs = refs[: sets * blocks]
+        right_refs = refs[sets * blocks : sets * blocks + sets]
+        add_refs = refs[sets * blocks + sets : sets * blocks + sets + len(adds)]
+        out_ref = refs[sets * blocks + sets + len(adds)]
+        turned = refs[sets * blocks + sets + len(adds) + 1 :]
+
+        @pl.when(pl.program_id(0) == 0)
+        def _():
+            for k in range(sets):
+                for b in range(blocks):
+                    turned[k][pl.ds(b * block, block), :] = left_refs[k * blocks + b][...].T
+
+        total = jnp.dot(turned[0][...], right_refs[0][...], preferred_element_type=jnp.float32)
+        for k in range(1, sets):
+            total += jnp.dot(turned[k][...], right_refs[k][...], preferred_element_type=jnp.float32)
+        for add_ref in add_refs:
+            total += add_ref[...].astype(jnp.float32)
+        out_ref[...] = total.astype(out_ref.dtype)
+
+    def left_spec(k, b):
+        return pl.BlockSpec((rows[k], block), lambda f, order_ref: (0, order_ref[b]))
+
+    in_specs = [left_spec(k, b) for k in range(sets) for b in range(blocks)]
+    in_specs += [
+        pl.BlockSpec((rows[k], tile), lambda f, order_ref, at=first_col // tile: (0, at + f))
+        for k, (_, first_col) in enumerate(rights)
+    ]
+    in_specs += [
+        pl.BlockSpec((blocks * block, tile), lambda f, order_ref, at=group: (at, f))
+        for _, group in adds
+    ]
+    depth = sum(rows)
+    return pl.pallas_call(
+        kernel,
+        out_shape=jax.ShapeDtypeStruct((blocks * block, width), kind),
+        grid_spec=pltpu.PrefetchScalarGridSpec(
+            num_scalar_prefetch=1,
+            grid=(width // tile,),
+            in_specs=in_specs,
+            out_specs=pl.BlockSpec((blocks * block, tile), lambda f, order_ref: (0, f)),
+            scratch_shapes=[pltpu.VMEM((blocks * block, count), jnp.bfloat16) for count in rows],
+        ),
+        compiler_params=pltpu.CompilerParams(dimension_semantics=("arbitrary",)),
+        cost_estimate=pl.CostEstimate(
+            flops=2 * depth * blocks * block * width,
+            bytes_accessed=2 * depth * (blocks * block + width)
+            + (4 if kind == jnp.float32 else 2) * blocks * block * width * (1 + len(adds)),
+            transcendentals=0,
+        ),
+    )(
+        order,
+        *[lefts[k] for k in range(sets) for _ in range(blocks)],
+        *[right for right, _ in rights],
+        *[add for add, _ in adds],
+    )
+
+
+def mlp_units(hidden, d_mlp, gate_up_weight, down_weight):
+    rows, model_width = hidden.shape
+    units = down_weight.shape[0]
+    tile = min(256, units)
+
+    def kernel(hidden_ref, d_mlp_ref, gate_ref, up_ref, down_ref, d_gate_ref, d_up_ref, swiglu_ref):
+        gate = jnp.dot(hidden_ref[...], gate_ref[...], preferred_element_type=jnp.float32)
+        up = jnp.dot(hidden_ref[...], up_ref[...], preferred_element_type=jnp.float32)
+        d_swiglu = lax.dot_general(
+            d_mlp_ref[...],
+            down_ref[...],
+            (((1,), (1,)), ((), ())),
+            preferred_element_type=jnp.float32,
+        )
+        sigmoid = jax.nn.sigmoid(gate)
+        silu = gate * sigmoid
+        swiglu_ref[...] = (silu * up).astype(jnp.bfloat16)
+        d_gate_ref[...] = (d_swiglu * up * sigmoid * (1.0 + gate * (1.0 - sigmoid))).astype(
+            jnp.bfloat16
+        )
+        d_up_ref[...] = (d_swiglu * silu).astype(jnp.bfloat16)
+
+    whole = pl.BlockSpec((rows, model_width), lambda f: (0, 0))
+    out = pl.BlockSpec((rows, tile), lambda f: (0, f))
+    return pl.pallas_call(
+        kernel,
+        out_shape=[jax.ShapeDtypeStruct((rows, units), jnp.bfloat16)] * 3,
+        grid=(units // tile,),
+        in_specs=[
+            whole,
+            whole,
+            pl.BlockSpec((None, model_width, tile), lambda f: (0, 0, f)),
+            pl.BlockSpec((None, model_width, tile), lambda f: (1, 0, f)),
+            pl.BlockSpec((tile, model_width), lambda f: (f, 0)),
+        ],
+        out_specs=[out, out, out],
+        compiler_params=pltpu.CompilerParams(dimension_semantics=("arbitrary",)),
+        cost_estimate=pl.CostEstimate(
+            flops=6 * rows * model_width * units,
+            bytes_accessed=2 * (2 * rows * model_width + 3 * model_width * units + 3 * rows * units),
+            transcendentals=rows * units,
+        ),
+    )(hidden, d_mlp, gate_up_weight, gate_up_weight, down_weight)
+
+
+def send_order(top):
+    def halves(codes, bit):
+        if len(codes) == 1:
+            return codes
+        return halves([c for c in codes if c & bit], 2 * bit) + halves(
+            [c for c in codes if not c & bit], 2 * bit
+        )
+
+    stages = []
+    bit = 1
+    while bit < top:
+        stages.append((bit, [bit + c for c in halves(list(range(0, top, 2 * bit)), 2 * bit)]))
+        bit *= 2
+    return stages
+
+
+def owners_sum(lefts, rights, width, top):
+    me = lax.axis_index("replica")
+    received = []
+
+    def part(codes, kind):
+        adds = [(array, held.index(codes[0]) // len(codes)) for array, held in received]
+        order = me ^ jnp.array(codes, jnp.int32)
+        return grad_blocks(order, lefts, rights, width, adds, kind)
+
+    for bit, codes in send_order(top):
+        sent = part(codes, jnp.bfloat16)
+        received.append((exchange(sent, "replica", bit), [code ^ bit for code in codes]))
+    return part([0], jnp.float32)
+
+
+def weight_grads(saved, partner, qkv_width, units):
+    replicas = lax.axis_size("replica")
+    parts = [list(group) for group in zip(*saved)]
+    x_full, d_projected, context, d_attn, hidden, d_gate_up, swiglu, d_mlp = parts
+    far_hidden, far_d_mlp, far_d_gate, far_d_up, far_swiglu = partner
+    near = replicas // 2
+    down = owners_sum(
+        d_mlp + [far_d_mlp], [(own, 0) for own in swiglu] + [(far_swiglu, 0)], units, near
+    )
+    gate = owners_sum(
+        hidden + [far_hidden], [(own, 0) for own in d_gate_up] + [(far_d_gate, 0)], units, near
+    )
+    up = owners_sum(
+        hidden + [far_hidden], [(own, units) for own in d_gate_up] + [(far_d_up, 0)], units, near
+    )
+    out = owners_sum(d_attn, [(own, 0) for own in context], qkv_width, replicas)
+    qkv = owners_sum(x_full, [(own, 0) for own in d_projected], 3 * qkv_width, replicas)
+    qkv = jnp.stack([qkv[:, n * qkv_width : (n + 1) * qkv_width] for n in range(3)])
+    return (qkv, out.T, jnp.stack([gate, up]), down.T)
 
 
 def on_device(
@@ -302,8 +452,9 @@
     input_grads = []
     saved = []
     gains = []
+    d_mlp_rows = []
     for micro_idx in range(micro):
-        out_rows, input_rows, kept, gain_add, query_key_add = micro_step(
+        out_rows, input_rows, kept, d_mlp, gain_add, query_key_add = micro_step(
             tokens[micro_idx],
             cotangent[micro_idx],
             parents[micro_idx, 0],
@@ -318,8 +469,23 @@
         outputs.append(out_rows)
         input_grads.append(input_rows)
         saved.append(kept)
+        d_mlp_rows.append(d_mlp)
         gains.append((gain_add, query_key_add))
-    grads = weight_grads(saved)
+    far = lax.axis_size("replica") // 2
+    far_hidden = exchange(jnp.concatenate([kept[4] for kept in saved], axis=0), "replica", far)
+    far_rows = exchange(jnp.stack(d_mlp_rows), "replica", far)
+    far_d_mlp = jnp.concatenate(
+        [far_rows]
+        + [exchange(far_rows, "fsdp", flip) for flip in range(1, lax.axis_size("fsdp"))],
+        axis=1,
+    ).reshape(far_hidden.shape)
+    far_d_gate, far_d_up, far_swiglu = mlp_units(far_hidden, far_d_mlp, gate_up_weight, down_weight)
+    grads = weight_grads(
+        saved,
+        (far_hidden, far_d_mlp, far_d_gate, far_d_up, far_swiglu),
+        local_width,
+        down_weight.shape[0],
+    )
     gain_rows = sum(gain for gain, _ in gains)
     query_key_rows = sum(gain for _, gain in gains)
     size = lax.axis_size("fsdp")

time: 696 us -> 597 us (0.86)
  waiting for transfers between devices: 345 us -> 120 us
  Pallas kernels: 0 us -> 109 us
  other arithmetic: 37.8 us -> 65.8 us
  matrix products: 127 us -> 107 us
  starting transfers between devices: 82.5 us -> 97.4 us
  between operations: 16.4 us -> 2.94 us
    reduce_scatter x4 -> x0, waiting for transfers between devices: 261 us -> none  [to_owners(): lax.psum_scatter(grad, 'replica', scatter_dimension=dim, tiled=True)]
    pallas_call x0 -> x18, Pallas kernels: none -> 109 us  [the longest x17 88.8 us: grad_blocks(): pl.pallas_call(kernel, out_shape=jax.ShapeDtypeStruct((blocks * block, wi...]
    ppermute x66 -> x83, waiting for transfers between devices: 83.9 us -> 120 us  [exchange(): return lax.ppermute(value, axis, [(i, i ^ flip) for i in range(size)])]
    dot_general x4 -> x0, matrix products: 34.3 us -> none  [the longest x1 14.7 us: weight_grads(): jnp.einsum('td,tnf->ndf', hidden, d_gate_up, preferred_element_type=kind)]
    convert_element_type x0 -> x8, local copies, waits for them, and re-layouts: none -> 19.2 us  [the longest x4 16.4 us: micro_step(): d_gate_up = jnp.stack([d_gate, d_up], axis=1).astype(jnp.bfloat16)]
    concatenate x0 -> x9, other arithmetic: none -> 16.4 us  [the longest x8 13.3 us: gather_rows(): jnp.concatenate([rows] + [exchange(rows, 'fsdp', flip) for flip in range(...]
    unnamed x312 -> x291, local copies, waits for them, and re-layouts: 33.6 us -> 17.9 us
    ppermute x66 -> x83, starting transfers between devices: 82.1 us -> 97.4 us  [exchange(): return lax.ppermute(value, axis, [(i, i ^ flip) for i in range(size)])]
  transfers between devices with their start and end apart: 70 -> 83, of which waited for: 29 -> 16; matrix products, arithmetic and copies ran while one was open for 28% -> 39% of each run, Pallas kernels for 0% -> 18%
where the time goes in v2:
time: 597 us; the launch traced here: 585 us
  waiting for transfers between devices  120 us (20%)
  Pallas kernels  109 us (18%)
  matrix products  107 us (18%)
  starting transfers between devices  97.4 us (16%)
  local copies, waits for them, and re-layouts  82.2 us (14%)
  other arithmetic  65.8 us (11%)
    ppermute x83, waiting for transfers between devices, exchange(): return lax.ppermute(value, axis, [(i, i ^ flip) for i in range(size)])  120 us
    ppermute x83, starting transfers between devices, exchange(): return lax.ppermute(value, axis, [(i, i ^ flip) for i in range(size)])  97.4 us
    pallas_call x17, Pallas kernels, grad_blocks(): pl.pallas_call(kernel, out_shape=jax.ShapeDtypeStruct((blocks * block, wi...  88.8 us
    dot_general x2, matrix products, micro_step(): jnp.einsum('tnf,ndf->td', d_gate_up, gate_up_weight, preferred_element_ty...  23.9 us
    pallas_call x1, Pallas kernels, mlp_units(): pl.pallas_call(kernel, out_shape=[jax.ShapeDtypeStruct((rows, units), jnp...  20.7 us
    unnamed x291, local copies, waits for them, and re-layouts  17.9 us
    dot_general x2, matrix products, micro_step(): jnp.einsum('td,fd->tf', d_mlp_full, down_weight, preferred_element_type=j...  17.2 us
    dot_general x2, matrix products, micro_step(): jnp.einsum('td,ndf->tnf', hidden_full, gate_up_weight, preferred_element_...  16.7 us
  transfers between devices with their start and end apart: 83, of which 16 were waited for; matrix products, arithmetic and copies ran while one was open for 39% of the time, Pallas kernels for 18%

profile of v2, /device:TPU:0, one launch (start us, length us, event | category | flops | bytes accessed | tf_op | source)
XLA Modules:
  0.0 585.1 jit_solution(9621890812738163639)
XLA Ops:
  95.9 5.8 collective-permute-done.9
  105.9 8.1 %fusion.14 = f32[256,2,2048]{2,0,1:T(8,128)S(1)} fusion(bf16[2,2048,2048]{2,1,0:T(8,128)(2,1)} %up_ref.1, bf16[64,2048]{1,0:T(8,128)(2,1)S(1)} %collective-permute-done.11, bf16[64,2048]{1,0:T(8,128)(2,1)S(1)} %collective-permute-done.10, bf16[64,2048]{1,0:T(8,128)(2,1)S(1)} %collective-permute-done.9, bf16[64,2048]{1,0:T(8,128)(2,1)S(1)} %get-tuple-element.69), kind=kOutput, calls=%fused_computation.65 | convolution fusion | flops 4299161600 | bytes 22020096 | tf_op jit(solution)/shard_map/td,ndf->tnf/dot_general | solution.py:173
  114.7 6.1 %fusion.149 = bf16[256,2048]{1,0:T(8,128)(2,1)S(1)} fusion(bf16[256,2048]{1,0:T(8,128)(2,1)S(1)} %multiply_convert_fusion.1.refs_6_.refs_3_, bf16[2048,2048]{1,0:T(8,128)(2,1)} %down_ref.1), kind=kOutput, calls=%fused_computation.351 | convolution fusion | flops 2147483648 | bytes 10485760 | tf_op jit(solution)/shard_map/dot_general | solution.py:181
  125.6 8.6 %fusion.10 = f32[256,2,2048]{2,0,1:T(8,128)S(1)} fusion(bf16[2,2048,2048]{2,1,0:T(8,128)(2,1)} %up_ref.1, bf16[64,2048]{1,0:T(8,128)(2,1)S(1)} %collective-permute-done.26, bf16[64,2048]{1,0:T(8,128)(2,1)S(1)} %collective-permute-done.25, bf16[64,2048]{1,0:T(8,128)(2,1)S(1)} %collective-permute-done.24, bf16[64,2048]{1,0:T(8,128)(2,1)S(1)} %get-tuple-element.67), kind=kOutput, calls=%fused_computation.61 | convolution fusion | flops 4299161600 | bytes 22020096 | tf_op jit(solution)/shard_map/td,ndf->tnf/dot_general | solution.py:173
  136.1 6.1 %fusion.151 = bf16[256,2048]{1,0:T(8,128)(2,1)S(1)} fusion(bf16[256,2048]{1,0:T(8,128)(2,1)S(1)} %multiply_convert_fusion.refs_7_.refs_4_, bf16[2048,2048]{1,0:T(8,128)(2,1)} %down_ref.1), kind=kOutput, calls=%fused_computation.353 | convolution fusion | flops 2147483648 | bytes 10485760 | tf_op jit(solution)/shard_map/dot_general | solution.py:181
  169.3 7.9 %multiply_bitcast_fusion.3 = (bf16[256,1,2048]{2,0,1:T(8,128)(2,1)}, bf16[256,1,2048]{2,0,1:T(8,128)(2,1)}) fusion(f32[256,2,2048]{2,0,1:T(8,128)S(1)} %fusion.14, bf16[2048,2048]{1,0:T(8,128)(2,1)} %down_ref.1, bf16[64,2048]{1,0:T(8,128)(2,1)S(1)} %collective-permute-done.32, bf16[64,2048]{1,0:T(8,128)(2,1)S(1)} %collective-permute-done.31, ...), kind=kOutput, calls=%fused_computation.15 | convolution fusion | flops 2158493696 | bytes 15728640 | tf_op jit(solution)/shard_map/td,fd->tf/dot_general | solution.py:195
  177.3 11.9 %convolution_bitcast_fusion.1 = bf16[256,2048]{1,0:T(8,128)(2,1)} fusion(bf16[2,2048,2048]{2,1,0:T(8,128)(2,1)} %up_ref.1, bf16[256,1,2048]{2,0,1:T(8,128)(2,1)} %get-tuple-element.85, bf16[256,1,2048]{2,0,1:T(8,128)(2,1)} %get-tuple-element.84), kind=kOutput, calls=%fused_computation.4 | convolution fusion | flops 4296015872 | bytes 19922944 | tf_op jit(solution)/shard_map/tnf,ndf->td/dot_general | solution.py:200
  195.0 9.3 %multiply_bitcast_fusion.1 = (bf16[256,1,2048]{2,0,1:T(8,128)(2,1)}, bf16[256,1,2048]{2,0,1:T(8,128)(2,1)}) fusion(f32[256,2,2048]{2,0,1:T(8,128)} %copy-done.28, bf16[2048,2048]{1,0:T(8,128)(2,1)} %down_ref.1, bf16[64,2048]{1,0:T(8,128)(2,1)} %collective-permute-done.47, bf16[64,2048]{1,0:T(8,128)(2,1)} %collective-permute-done.46, ...), kind=kOutput, calls=%fused_computation.13 | convolution fusion | flops 2158493696 | bytes 15728640 | tf_op jit(solution)/shard_map/td,fd->tf/dot_general | solution.py:195
  204.2 11.9 %convolution_bitcast_fusion = bf16[256,2048]{1,0:T(8,128)(2,1)} fusion(bf16[2,2048,2048]{2,1,0:T(8,128)(2,1)} %up_ref.1, bf16[256,1,2048]{2,0,1:T(8,128)(2,1)} %get-tuple-element.87, bf16[256,1,2048]{2,0,1:T(8,128)(2,1)} %get-tuple-element.86), kind=kOutput, calls=%fused_computation.3 | convolution fusion | flops 4296015872 | bytes 19922944 | tf_op jit(solution)/shard_map/tnf,ndf->td/dot_general | solution.py:200
  337.7 6.2 %shard_map.314 = bf16[1024,1536]{1,0:T(8,128)(2,1)} custom-call(s32[4]{0:T(128)} %broadcast_xor_fusion.2.order_ref, bf16[256,2048]{1,0:T(8,128)(2,1)} %pad_maximum_fusion.3.refs_0_.refs_1_.refs_2_.refs_3_, bf16[256,2048]{1,0:T(8,128)(2,1)} %pad_maximum_fusion.3.refs_0_.refs_1_.refs_2_.refs_3_, ...), custom_call_target="tpu_custom_call" | custom-call | flops 1610612736 | bytes 5767168 | tf_op jit(solution)/shard_map/pallas_call | solution.py:315
  351.7 20.7 %shard_map.322 = (bf16[512,2048]{1,0:T(8,128)(2,1)}, bf16[512,2048]{1,0:T(8,128)(2,1)}, bf16[512,2048]{1,0:T(8,128)(2,1)}) custom-call(bf16[512,2048]{1,0:T(8,128)(2,1)} %collective-permute-done.66.hidden_ref.refs_4_.refs_5_.refs_2_, bf16[512,2048]{1,0:T(8,128)(2,1)} %bitcast.388, bf16[2,2048,2048]{2,1,0:T(8,128)(2,1)} %up_ref.1, ...), custom_call_target="tpu_custom_call" | custom-call | flops 12884901888 | bytes 35651584 | tf_op jit(solution)/shard_map/pallas_call | solution.py:364
  372.4 7.2 %shard_map.326 = bf16[512,2048]{1,0:T(8,128)(2,1)} custom-call(s32[2]{0:T(128)} %broadcast_xor_fusion.order_ref, bf16[256,2048]{1,0:T(8,128)(2,1)} %pad_maximum_fusion.4.refs_0_.refs_1_, bf16[256,2048]{1,0:T(8,128)(2,1)} %pad_maximum_fusion.4.refs_0_.refs_1_, bf16[256,2048]{1,0:T(8,128)(2,1)} %pad_maximum_fusion.6.refs_2_.refs_3_.refs_1_, ...), custom_call_target="tpu_custom_call" | custom-call | flops 2147483648 | bytes 7340032 | tf_op jit(solution)/shard_map/pallas_call | solution.py:315
  379.5 7.1 %shard_map.323 = bf16[512,2048]{1,0:T(8,128)(2,1)} custom-call(s32[2]{0:T(128)} %broadcast_xor_fusion.order_ref, bf16[256,2048]{1,0:T(8,128)(2,1)} %pad_maximum_fusion.4.refs_0_.refs_1_, bf16[256,2048]{1,0:T(8,128)(2,1)} %pad_maximum_fusion.4.refs_0_.refs_1_, bf16[256,2048]{1,0:T(8,128)(2,1)} %pad_maximum_fusion.6.refs_2_.refs_3_.refs_1_, ...), custom_call_target="tpu_custom_call" | custom-call | flops 2147483648 | bytes 7340032 | tf_op jit(solution)/shard_map/pallas_call | solution.py:315
  387.2 7.1 %shard_map.329 = bf16[512,2048]{1,0:T(8,128)(2,1)} custom-call(s32[2]{0:T(128)} %broadcast_xor_fusion.order_ref, bf16[256,2048]{1,0:T(8,128)(2,1)} %pad_maximum_fusion.8.refs_0_.refs_1_, bf16[256,2048]{1,0:T(8,128)(2,1)} %pad_maximum_fusion.8.refs_0_.refs_1_, bf16[256,2048]{1,0:T(8,128)(2,1)} %pad_maximum_fusion.10.refs_2_.refs_3_.refs_1_, ...), custom_call_target="tpu_custom_call" | custom-call | flops 2147483648 | bytes 7340032 | tf_op jit(solution)/shard_map/pallas_call | solution.py:315
  402.3 5.6 convolution_bitcast_fusion.3
  407.9 5.5 shard_map.315
  432.0 5.5 shard_map.324
  437.4 5.5 shard_map.330
  450.5 12.5 %collective-permute-done.64.refs_5_ = bf16[512,512]{1,0:T(8,128)(2,1)S(1)} collective-permute-done((bf16[512,512]{1,0:T(8,128)(2,1)}, bf16[512,512]{1,0:T(8,128)(2,1)S(1)}, u32[]{:S(2)}, u32[]{:S(2)}) %collective-permute-start.64) | collective-permute-done | bytes 524320 | tf_op jit(solution)/shard_map/ppermute | solution.py:17
  475.5 58.4 %collective-permute-done.65.refs_6_ = bf16[256,512]{1,0:T(8,128)(2,1)S(1)} collective-permute-done((bf16[256,512]{1,0:T(8,128)(2,1)}, bf16[256,512]{1,0:T(8,128)(2,1)S(1)}, u32[]{:S(2)}, u32[]{:S(2)}) %collective-permute-start.65) | collective-permute-done | bytes 262176 | tf_op jit(solution)/shard_map/ppermute | solution.py:17
  539.2 12.7 %collective-permute-done.76.refs_7_ = bf16[256,2048]{1,0:T(8,128)(2,1)} collective-permute-done((bf16[256,2048]{1,0:T(8,128)(2,1)}, bf16[256,2048]{1,0:T(8,128)(2,1)}, u32[]{:S(2)}, u32[]{:S(2)}) %collective-permute-start.76) | collective-permute-done | bytes 1048608 | tf_op jit(solution)/shard_map/ppermute | solution.py:17
  552.0 5.9 %shard_map.331 = f32[256,2048]{1,0:T(8,128)} custom-call(s32[1]{0:T(128)} %bitcast.116.order_ref, bf16[256,2048]{1,0:T(8,128)(2,1)} %pad_maximum_fusion.8.refs_0_.refs_1_, bf16[256,2048]{1,0:T(8,128)(2,1)} %pad_maximum_fusion.10.refs_2_.refs_3_.refs_1_, bf16[512,2048]{1,0:T(8,128)(2,1)} %bitcast.392, bf16[256,2048]{1,0:T(8,128)(2,1)} %copy-done.6, ...), custom_call_target="tpu_custom_call" | custom-call | flops 1073741824 | bytes 11010048 | tf_op jit(solution)/shard_map/pallas_call | solution.py:315
  560.7 5.9 %shard_map.328 = f32[256,2048]{1,0:T(8,128)} custom-call(s32[1]{0:T(128)} %bitcast.116.order_ref, bf16[256,2048]{1,0:T(8,128)(2,1)} %pad_maximum_fusion.4.refs_0_.refs_1_, bf16[256,2048]{1,0:T(8,128)(2,1)} %pad_maximum_fusion.6.refs_2_.refs_3_.refs_1_, bf16[512,2048]{1,0:T(8,128)(2,1)} %collective-permute-done.66.hidden_ref.refs_4_.refs_5_.refs_2_, ...), custom_call_target="tpu_custom_call" | custom-call | flops 1073741824 | bytes 11010048 | tf_op jit(solution)/shard_map/pallas_call | solution.py:315
  566.6 6.1 %shard_map.325 = f32[256,2048]{1,0:T(8,128)} custom-call(s32[1]{0:T(128)} %bitcast.116.order_ref, bf16[256,2048]{1,0:T(8,128)(2,1)} %pad_maximum_fusion.4.refs_0_.refs_1_, bf16[256,2048]{1,0:T(8,128)(2,1)} %pad_maximum_fusion.6.refs_2_.refs_3_.refs_1_, bf16[512,2048]{1,0:T(8,128)(2,1)} %collective-permute-done.66.hidden_ref.refs_4_.refs_5_.refs_2_, ...), custom_call_target="tpu_custom_call" | custom-call | flops 1073741824 | bytes 11010048 | tf_op jit(solution)/shard_map/pallas_call | solution.py:315
  (654 shorter events, 334.6 us)
Async XLA Ops:
  159.1 35.1 %collective-permute-start.47 = (bf16[64,2048]{1,0:T(8,128)(2,1)}, bf16[64,2048]{1,0:T(8,128)(2,1)}, u32[]{:S(2)}, u32[]{:S(2)}) collective-permute-start(bf16[64,2048]{1,0:T(8,128)(2,1)} %get-tuple-element.133), channel_id=1, source_target_pairs={{0,3},{1,2},{2,1},{3,0},{4,7},{5,6},{6,5},{7,4},{8,11},{9,10},{10,... | collective-permute-start | bytes 786440 | tf_op jit(solution)/shard_map/ppermute | solution.py:17
  161.8 33.1 %collective-permute-start.46 = (bf16[64,2048]{1,0:T(8,128)(2,1)}, bf16[64,2048]{1,0:T(8,128)(2,1)}, u32[]{:S(2)}, u32[]{:S(2)}) collective-permute-start(bf16[64,2048]{1,0:T(8,128)(2,1)} %get-tuple-element.133), channel_id=1, source_target_pairs={{0,2},{1,3},{2,0},{3,1},{4,6},{5,7},{6,4},{7,5},{8,10},{9,11},{10,... | collective-permute-start | bytes 786440 | tf_op jit(solution)/shard_map/ppermute | solution.py:17
  165.7 29.2 %collective-permute-start.45 = (bf16[64,2048]{1,0:T(8,128)(2,1)}, bf16[64,2048]{1,0:T(8,128)(2,1)}, u32[]{:S(2)}, u32[]{:S(2)}) collective-permute-start(bf16[64,2048]{1,0:T(8,128)(2,1)} %get-tuple-element.133), channel_id=1, source_target_pairs={{0,1},{1,0},{2,3},{3,2},{4,5},{5,4},{6,7},{7,6},{8,9},{9,8},{10,11... | collective-permute-start | bytes 786440 | tf_op jit(solution)/shard_map/ppermute | solution.py:17
  191.2 31.8 %collective-permute-start.35 = (bf16[64,2048]{1,0:T(8,128)(2,1)}, bf16[64,2048]{1,0:T(8,128)(2,1)}, u32[]{:S(2)}, u32[]{:S(2)}) collective-permute-start(bf16[64,2048]{1,0:T(8,128)(2,1)} %get-tuple-element.103), channel_id=1, source_target_pairs={{0,3},{1,2},{2,1},{3,0},{4,7},{5,6},{6,5},{7,4},{8,11},{9,10},{10,... | collective-permute-start | bytes 786440 | tf_op jit(solution)/shard_map/ppermute | solution.py:17
  193.5 33.0 %collective-permute-start.34 = (bf16[64,2048]{1,0:T(8,128)(2,1)}, bf16[64,2048]{1,0:T(8,128)(2,1)}, u32[]{:S(2)}, u32[]{:S(2)}) collective-permute-start(bf16[64,2048]{1,0:T(8,128)(2,1)} %get-tuple-element.104), channel_id=1, source_target_pairs={{0,2},{1,3},{2,0},{3,1},{4,6},{5,7},{6,4},{7,5},{8,10},{9,11},{10,... | collective-permute-start | bytes 786440 | tf_op jit(solution)/shard_map/ppermute | solution.py:17
  194.2 35.0 %collective-permute-start.33 = (bf16[64,2048]{1,0:T(8,128)(2,1)}, bf16[64,2048]{1,0:T(8,128)(2,1)}, u32[]{:S(2)}, u32[]{:S(2)}) collective-permute-start(bf16[64,2048]{1,0:T(8,128)(2,1)} %get-tuple-element.102), channel_id=1, source_target_pairs={{0,1},{1,0},{2,3},{3,2},{4,5},{5,4},{6,7},{7,6},{8,9},{9,8},{10,11... | collective-permute-start | bytes 786440 | tf_op jit(solution)/shard_map/ppermute | solution.py:17
  226.5 39.6 %collective-permute-start.67 = (bf16[2,64,2048]{2,1,0:T(8,128)(2,1)}, bf16[2,64,2048]{2,1,0:T(8,128)(2,1)}, u32[]{:S(2)}, u32[]{:S(2)}) collective-permute-start(bf16[2,64,2048]{2,1,0:T(8,128)(2,1)} %pad_maximum_fusion.13), channel_id=1, source_target_pairs={{0,16},{4,20},{8,24},{12,28},{16,0},{20,4},{24,8},{28,12},{1,17},{... | collective-permute-start | bytes 1572872 | tf_op jit(solution)/shard_map/ppermute | solution.py:17
  239.3 28.9 %collective-permute-start.53 = (bf16[64,2048]{1,0:T(8,128)(2,1)}, bf16[64,2048]{1,0:T(8,128)(2,1)}, u32[]{:S(2)}, u32[]{:S(2)}) collective-permute-start(bf16[64,2048]{1,0:T(8,128)(2,1)} %get-tuple-element.182), channel_id=1, source_target_pairs={{0,3},{1,2},{2,1},{3,0},{4,7},{5,6},{6,5},{7,4},{8,11},{9,10},{10,... | collective-permute-start | bytes 786440 | tf_op jit(solution)/shard_map/ppermute | solution.py:17
  240.9 28.7 %collective-permute-start.51 = (bf16[64,2048]{1,0:T(8,128)(2,1)}, bf16[64,2048]{1,0:T(8,128)(2,1)}, u32[]{:S(2)}, u32[]{:S(2)}) collective-permute-start(bf16[64,2048]{1,0:T(8,128)(2,1)} %get-tuple-element.182), channel_id=1, source_target_pairs={{0,1},{1,0},{2,3},{3,2},{4,5},{5,4},{6,7},{7,6},{8,9},{9,8},{10,11... | collective-permute-start | bytes 786440 | tf_op jit(solution)/shard_map/ppermute | solution.py:17
  262.6 89.1 %collective-permute-start.66 = (bf16[512,2048]{1,0:T(8,128)(2,1)}, bf16[512,2048]{1,0:T(8,128)(2,1)}, u32[]{:S(2)}, u32[]{:S(2)}) collective-permute-start(bf16[512,2048]{1,0:T(8,128)(2,1)} %copy-done.100), channel_id=1, source_target_pairs={{0,16},{4,20},{8,24},{12,28},{16,0},{20,4},{24,8},{28,12},{1,17},{... | collective-permute-start | bytes 6291464 | tf_op jit(solution)/shard_map/ppermute | solution.py:17
  269.7 78.5 %collective-permute-start.70 = (bf16[2,64,2048]{2,1,0:T(8,128)(2,1)}, bf16[2,64,2048]{2,1,0:T(8,128)(2,1)}, u32[]{:S(2)}, u32[]{:S(2)}) collective-permute-start(bf16[2,64,2048]{2,1,0:T(8,128)(2,1)} %collective-permute-done.67), channel_id=1, source_target_pairs={{0,3},{1,2},{2,1},{3,0},{4,7},{5,6},{6,5},{7,4},{8,11},{9,10},{10,... | collective-permute-start | bytes 1572872 | tf_op jit(solution)/shard_map/ppermute | solution.py:17
  280.0 68.6 %collective-permute-start.69 = (bf16[2,64,2048]{2,1,0:T(8,128)(2,1)}, bf16[2,64,2048]{2,1,0:T(8,128)(2,1)}, u32[]{:S(2)}, u32[]{:S(2)}) collective-permute-start(bf16[2,64,2048]{2,1,0:T(8,128)(2,1)} %collective-permute-done.67), channel_id=1, source_target_pairs={{0,2},{1,3},{2,0},{3,1},{4,6},{5,7},{6,4},{7,5},{8,10},{9,11},{10,... | collective-permute-start | bytes 1572872 | tf_op jit(solution)/shard_map/ppermute | solution.py:17
  280.6 67.9 %collective-permute-start.68 = (bf16[2,64,2048]{2,1,0:T(8,128)(2,1)}, bf16[2,64,2048]{2,1,0:T(8,128)(2,1)}, u32[]{:S(2)}, u32[]{:S(2)}) collective-permute-start(bf16[2,64,2048]{2,1,0:T(8,128)(2,1)} %collective-permute-done.67), channel_id=1, source_target_pairs={{0,1},{1,0},{2,3},{3,2},{4,5},{5,4},{6,7},{7,6},{8,9},{9,8},{10,11... | collective-permute-start | bytes 1572872 | tf_op jit(solution)/shard_map/ppermute | solution.py:17
  343.9 56.9 %collective-permute-start.60 = (bf16[1024,1536]{1,0:T(8,128)(2,1)}, bf16[1024,1536]{1,0:T(8,128)(2,1)S(1)}, u32[]{:S(2)}, u32[]{:S(2)}) collective-permute-start(bf16[1024,1536]{1,0:T(8,128)(2,1)} %shard_map.314), channel_id=1, source_target_pairs={{0,4},{4,0},{8,12},{12,8},{16,20},{20,16},{24,28},{28,24},{1,5},{5... | collective-permute-start | bytes 9437192 | tf_op jit(solution)/shard_map/ppermute | solution.py:17
  348.1 51.2 %collective-permute-start.82 = (f32[4,512]{1,0:T(4,128)S(1)}, f32[4,512]{1,0:T(4,128)S(1)}, u32[]{:S(2)}, u32[]{:S(2)}) collective-permute-start(f32[4,512]{1,0:T(4,128)S(1)} %add.398), channel_id=1, source_target_pairs={{0,16},{4,20},{8,24},{12,28},{16,0},{20,4},{24,8},{28,12},{1,17},{... | collective-permute-start | bytes 24584 | tf_op jit(solution)/shard_map/ppermute | solution.py:17
  379.5 43.5 %collective-permute-start.73 = (bf16[512,2048]{1,0:T(8,128)(2,1)}, bf16[512,2048]{1,0:T(8,128)(2,1)}, u32[]{:S(2)}, u32[]{:S(2)}) collective-permute-start(bf16[512,2048]{1,0:T(8,128)(2,1)} %shard_map.326), channel_id=1, source_target_pairs={{0,4},{4,0},{8,12},{12,8},{16,20},{20,16},{24,28},{28,24},{1,5},{5... | collective-permute-start | bytes 6291464 | tf_op jit(solution)/shard_map/ppermute | solution.py:17
  386.7 37.7 %collective-permute-start.71 = (bf16[512,2048]{1,0:T(8,128)(2,1)}, bf16[512,2048]{1,0:T(8,128)(2,1)}, u32[]{:S(2)}, u32[]{:S(2)}) collective-permute-start(bf16[512,2048]{1,0:T(8,128)(2,1)} %shard_map.323), channel_id=1, source_target_pairs={{0,4},{4,0},{8,12},{12,8},{16,20},{20,16},{24,28},{28,24},{1,5},{5... | collective-permute-start | bytes 6291464 | tf_op jit(solution)/shard_map/ppermute | solution.py:17
  394.3 30.9 %collective-permute-start.75 = (bf16[512,2048]{1,0:T(8,128)(2,1)}, bf16[512,2048]{1,0:T(8,128)(2,1)}, u32[]{:S(2)}, u32[]{:S(2)}) collective-permute-start(bf16[512,2048]{1,0:T(8,128)(2,1)} %shard_map.329), channel_id=1, source_target_pairs={{0,4},{4,0},{8,12},{12,8},{16,20},{20,16},{24,28},{28,24},{1,5},{5... | collective-permute-start | bytes 6291464 | tf_op jit(solution)/shard_map/ppermute | solution.py:17
  414.3 54.5 %collective-permute-start.61 = (bf16[512,1536]{1,0:T(8,128)(2,1)}, bf16[512,1536]{1,0:T(8,128)(2,1)S(1)}, u32[]{:S(2)}, u32[]{:S(2)}) collective-permute-start(bf16[512,1536]{1,0:T(8,128)(2,1)} %shard_map.315), channel_id=1, source_target_pairs={{0,8},{4,12},{8,0},{12,4},{16,24},{20,28},{24,16},{28,20},{1,9},{5... | collective-permute-start | bytes 4718600 | tf_op jit(solution)/shard_map/ppermute | solution.py:17
  443.6 117.2 %collective-permute-start.74 = (bf16[256,2048]{1,0:T(8,128)(2,1)}, bf16[256,2048]{1,0:T(8,128)(2,1)}, u32[]{:S(2)}, u32[]{:S(2)}) collective-permute-start(bf16[256,2048]{1,0:T(8,128)(2,1)} %shard_map.327), channel_id=1, source_target_pairs={{0,8},{4,12},{8,0},{12,4},{16,24},{20,28},{24,16},{28,20},{1,9},{5... | collective-permute-start | bytes 3145736 | tf_op jit(solution)/shard_map/ppermute | solution.py:17
  445.0 121.6 %collective-permute-start.72 = (bf16[256,2048]{1,0:T(8,128)(2,1)}, bf16[256,2048]{1,0:T(8,128)(2,1)}, u32[]{:S(2)}, u32[]{:S(2)}) collective-permute-start(bf16[256,2048]{1,0:T(8,128)(2,1)} %shard_map.324), channel_id=1, source_target_pairs={{0,8},{4,12},{8,0},{12,4},{16,24},{20,28},{24,16},{28,20},{1,9},{5... | collective-permute-start | bytes 3145736 | tf_op jit(solution)/shard_map/ppermute | solution.py:17
  445.6 106.4 %collective-permute-start.76 = (bf16[256,2048]{1,0:T(8,128)(2,1)}, bf16[256,2048]{1,0:T(8,128)(2,1)}, u32[]{:S(2)}, u32[]{:S(2)}) collective-permute-start(bf16[256,2048]{1,0:T(8,128)(2,1)} %shard_map.330), channel_id=1, source_target_pairs={{0,8},{4,12},{8,0},{12,4},{16,24},{20,28},{24,16},{28,20},{1,9},{5... | collective-permute-start | bytes 3145736 | tf_op jit(solution)/shard_map/ppermute | solution.py:17
  466.2 67.8 %collective-permute-start.65 = (bf16[256,512]{1,0:T(8,128)(2,1)}, bf16[256,512]{1,0:T(8,128)(2,1)S(1)}, u32[]{:S(2)}, u32[]{:S(2)}) collective-permute-start(bf16[256,512]{1,0:T(8,128)(2,1)} %shard_map.320), channel_id=1, source_target_pairs={{0,16},{4,20},{8,24},{12,28},{16,0},{20,4},{24,8},{28,12},{1,17},{... | collective-permute-start | bytes 786440 | tf_op jit(solution)/shard_map/ppermute | solution.py:17
  474.1 102.8 %collective-permute-start.62 = (bf16[256,1536]{1,0:T(8,128)(2,1)}, bf16[256,1536]{1,0:T(8,128)(2,1)}, u32[]{:S(2)}, u32[]{:S(2)}) collective-permute-start(bf16[256,1536]{1,0:T(8,128)(2,1)} %shard_map.316), channel_id=1, source_target_pairs={{0,16},{4,20},{8,24},{12,28},{16,0},{20,4},{24,8},{28,12},{1,17},{... | collective-permute-start | bytes 2359304 | tf_op jit(solution)/shard_map/ppermute | solution.py:17
  (201 other events, 2043.2 us)

commit v3 on v1

v3 whole, which is shorter than its diff:
```python
import jax
import jax.numpy as jnp
from jax import lax
from jax.experimental import pallas as pl
from jax.experimental.pallas import tpu as pltpu
from jax.sharding import PartitionSpec as P

HD = 128


EPSILON = 1e-06
ROPE_BASE = 500000.0
BF = jnp.bfloat16
F32 = jnp.float32


def exchange(value, axis, flip):
    size = lax.axis_size(axis)
    return lax.ppermute(value, axis, [(i, i ^ flip) for i in range(size)])


def gather_blocks(rows):
    return [rows] + [exchange(rows, "fsdp", flip) for flip in range(1, lax.axis_size("fsdp"))]


def swap_blocks(blocks):
    return [blocks[0]] + [exchange(blocks[flip], "fsdp", flip) for flip in range(1, len(blocks))]


def sum_small(value, axis):
    size = lax.axis_size(axis)
    flip = 1
    while flip < size:
        value = value + exchange(value, axis, flip)
        flip *= 2
    return value


def cost(flops, moved, transcendentals=0):
    return pl.CostEstimate(
        flops=int(flops), bytes_accessed=int(moved), transcendentals=int(transcendentals)
    )


def shape(dims, kind):
    return jax.ShapeDtypeStruct(dims, kind)


def dot(left, right):
    return jnp.dot(left, right, preferred_element_type=F32)


def dot_t(left, right):
    return lax.dot_general(left, right, (((1,), (1,)), ((), ())), preferred_element_type=F32)


def t_dot(left, right):
    return lax.dot_general(left, right, (((0,), (0,)), ((), ())), preferred_element_type=F32)


def lane_sums(field):
    ones = jnp.ones((8, field.shape[1]), F32)
    return lax.dot_general(
        ones,
        field,
        (((1,), (1,)), ((), ())),
        precision=lax.Precision.HIGHEST,
        preferred_element_type=F32,
    )


def join(block_refs, rows_ref):
    tok = block_refs[0].shape[0]
    for j, block_ref in enumerate(block_refs):
        rows_ref[pl.ds(j * tok, tok), :] = block_ref[...]


def write_blocks(rows, block_refs):
    tok = block_refs[0].shape[0]
    for j, block_ref in enumerate(block_refs):
        block_ref[...] = rows[j * tok : (j + 1) * tok].astype(block_ref.dtype)


def block_shapes(count, tok, width):
    return [shape((tok, width), F32)] + [shape((tok, width), BF)] * (count - 1)


def aligned_total(parts, tok):
    total = parts[0].T
    count = len(parts)
    for flip in range(1, count):
        column = parts[flip].T
        total = total + jnp.concatenate(
            [column[(j ^ flip) * tok : ((j ^ flip) + 1) * tok] for j in range(count)], axis=0
        )
    return total


def turn(field, cos_t, sin_t):
    return field * cos_t + pltpu.roll(field, HD // 2, 1) * sin_t


def turn_back(field, cos_t, sin_t):
    return field * cos_t - pltpu.roll(field, HD // 2, 1) * sin_t


VMEM = pl.BlockSpec(memory_space=pltpu.VMEM)
WHOLE = pltpu.CompilerParams(dimension_semantics=("arbitrary",))


def project(x_blocks, qkv_weight):
    count = len(x_blocks)
    tok, model_width = x_blocks[0].shape
    rows = count * tok
    width = qkv_weight.shape[2]

    def kernel(*refs):
        x_refs = refs[:count]
        weight_ref, raw_ref, values_ref, squares_ref, x_ref = refs[count:]
        step = pl.program_id(0)

        @pl.when(step == 0)
        def _():
            join(x_refs, x_ref)

        product = dot(x_ref[...], weight_ref[...])

        @pl.when(step < 2)
        def _():
            raw_ref[...] = product
            squares_ref[pl.ds(step, 1), :] = lane_sums(product * product)[:1]

        @pl.when(step == 2)
        def _():
            values_ref[...] = product.astype(BF)
            squares_ref[2:, :] = jnp.zeros((6, rows), F32)

    whole = pl.BlockSpec((tok, model_width), lambda n: (0, 0))
    return pl.pallas_call(
        kernel,
        out_shape=[
            shape((2, rows, width), F32),
            shape((rows, width), BF),
            shape((8, rows), F32),
            shape((rows, model_width), BF),
        ],
        grid=(3,),
        in_specs=[whole] * count + [pl.BlockSpec((None, model_width, width), lambda n: (n, 0, 0))],
        out_specs=[
            pl.BlockSpec((None, rows, width), lambda n: (jnp.minimum(n, 1), 0, 0)),
            pl.BlockSpec((rows, width), lambda n: (0, 0)),
            pl.BlockSpec((8, rows), lambda n: (0, 0)),
            pl.BlockSpec((rows, model_width), lambda n: (0, 0)),
        ],
        compiler_params=WHOLE,
        cost_estimate=cost(6 * rows * model_width * width, 6 * model_width * width + 8 * rows * width),
    )(*x_blocks, qkv_weight)


def attend(raw, values, squares, bias, cos_t, sin_t, qk_gain, out_weight):
    count = len(squares)
    _, rows, width = raw.shape
    heads = width // HD
    tok = rows // count
    model_width = out_weight.shape[1]
    total_width = model_width
    scale = HD ** (-0.5)

    def kernel(raw_ref, values_ref, bias_ref, cos_ref, sin_ref, gain_ref, out_weight_ref, *refs):
        parts = [ref[...] for ref in refs[:count]]
        context_ref, queries_ref, keys_ref, inv_ref = refs[count : count + 4]
        block_refs = refs[count + 4 :]
        inv = lax.rsqrt(aligned_total(parts, tok) / total_width + EPSILON)
        inv_ref[...] = inv
        cos_v, sin_v, bias_v = cos_ref[...], sin_ref[...], bias_ref[...]
        for h in range(heads):
            at = slice(h * HD, (h + 1) * HD)
            q = turn(raw_ref[0, :, at] * inv[:, 0:1] * gain_ref[0:1, at], cos_v, sin_v).astype(BF)
            k = turn(raw_ref[1, :, at] * inv[:, 1:2] * gain_ref[1:2, at], cos_v, sin_v).astype(BF)
            queries_ref[:, at] = q
            keys_ref[:, at] = k
            scores = dot_t(q, k) * scale + bias_v
            weights = jnp.exp(scores - jnp.max(scores, axis=1, keepdims=True))
            probs = (weights / jnp.sum(weights, axis=1, keepdims=True)).astype(BF)
            context_ref[:, at] = dot(probs, values_ref[:, at]).astype(BF)
        write_blocks(dot(context_ref[...], out_weight_ref[...]), block_refs)

    return pl.pallas_call(
        kernel,
        out_shape=[
            shape((rows, width), BF),
            shape((rows, width), BF),
            shape((rows, width), BF),
            shape((rows, 8), F32),
        ]
        + block_shapes(count, tok, model_width),
        in_specs=[VMEM] * (7 + count),
        out_specs=[VMEM] * (4 + count),
        cost_estimate=cost(
            4 * rows * rows * width + 2 * rows * width * model_width,
            2 * width * model_width + 14 * rows * width + 2 * rows * model_width,
            heads * rows * rows,
        ),
    )(raw, values, bias, cos_t, sin_t, qk_gain, out_weight, *squares)


def attend_back(
    d_attn_blocks, out_weight, queries, keys, values, raw, inv, bias, cos_t, sin_t, qk_gain
):
    count = len(d_attn_blocks)
    tok, model_width = d_attn_blocks[0].shape
    _, rows, width = raw.shape
    heads = width // HD
    scale = HD ** (-0.5)

    def kernel(*refs):
        (
            out_weight_ref,
            queries_ref,
            keys_ref,
            values_ref,
            raw_ref,
            inv_ref,
            bias_ref,
            cos_ref,
            sin_ref,
            gain_ref,
            d_attn_ref,
            d_norm_ref,
            d_values_ref,
            sums_ref,
            gain_sums_ref,
        ) = refs[count:]
        join(refs[:count], d_attn_ref)
        d_context = dot_t(d_attn_ref[...], out_weight_ref[...]).astype(BF)
        cos_v, sin_v, bias_v = cos_ref[...], sin_ref[...], bias_ref[...]
        inv = inv_ref[...]
        sums = [jnp.zeros((rows, HD), F32), jnp.zeros((rows, HD), F32)]
        for h in range(heads):
            at = slice(h * HD, (h + 1) * HD)
            q, k, v, d_out = queries_ref[:, at], keys_ref[:, at], values_ref[:, at], d_context[:, at]
            scores = dot_t(q, k) * scale + bias_v
            weights = jnp.exp(scores - jnp.max(scores, axis=1, keepdims=True))
            probs = weights / jnp.sum(weights, axis=1, keepdims=True)
            d_probs = dot_t(d_out, v)
            delta = jnp.sum(d_probs * probs, axis=1, keepdims=True)
            d_scores = (probs * (d_probs - delta)).astype(BF)
            d_values_ref[:, at] = t_dot(probs.astype(BF), d_out).astype(BF)
            turned = (dot(d_scores, k) * scale, t_dot(d_scores, q) * scale)
            for n in range(2):
                d_norm = turn_back(turned[n], cos_v, sin_v)
                d_norm_ref[n, :, at] = d_norm
                field = raw_ref[n, :, at] * d_norm
                sums[n] += field * gain_ref[n : n + 1, at]
                gain_sums_ref[n : n + 1, at] = jnp.sum(field * inv[:, n : n + 1], axis=0, keepdims=True)
        sums_ref[0:1, :] = lane_sums(sums[0])[:1]
        sums_ref[1:2, :] = lane_sums(sums[1])[:1]
        sums_ref[2:, :] = jnp.zeros((6, rows), F32)

    return pl.pallas_call(
        kernel,
        out_shape=[
            shape((rows, model_width), BF),
            shape((2, rows, width), F32),
            shape((rows, width), BF),
            shape((8, rows), F32),
            shape((2, width), F32),
        ],
        in_specs=[VMEM] * (10 + count),
        out_specs=[VMEM] * 5,
        cost_estimate=cost(
            10 * rows * rows * width + 2 * rows * width * model_width,
            2 * width * model_width + 24 * rows * width + 2 * rows * model_width,
            heads * rows * rows,
        ),
    )(
        *d_attn_blocks,
        out_weight,
        queries,
        keys,
        values,
        raw,
        inv,
        bias,
        cos_t,
        sin_t,
        qk_gain,
    )


def project_back(d_norm, d_values, raw, inv, sums, qk_gain, qkv_weight):
    count = len(sums)
    _, rows, width = raw.shape
    tok = rows // count
    model_width = qkv_weight.shape[1]

    def kernel(d_norm_ref, d_values_ref, raw_ref, inv_ref, gain_ref, weight_ref, *refs):
        parts = refs[:count]
        d_projected_ref = refs[count]
        block_refs = refs[count + 1 : 2 * count + 1]
        total_ref = refs[2 * count + 1]
        step = pl.program_id(0)
        inv = inv_ref[...]

        @pl.when(step == 0)
        def _():
            d_projected_ref[...] = d_values_ref[...]

        @pl.when(step > 0)
        def _():
            shared = aligned_total([part[...] for part in parts], tok)
            first = step == 1
            r = jnp.where(first, inv[:, 0:1], inv[:, 1:2])
            s = jnp.where(first, shared[:, 0:1], shared[:, 1:2])
            gain = jnp.where(first, gain_ref[0:1, :], gain_ref[1:2, :])
            d_projected_ref[...] = (
                r * (d_norm_ref[...] * gain) - raw_ref[...] * (r * r * r * s / model_width)
            ).astype(BF)

        product = dot_t(d_projected_ref[...], weight_ref[...])

        @pl.when(step == 0)
        def _():
            total_ref[...] = product

        @pl.when(step > 0)
        def _():
            total_ref[...] += product

        @pl.when(step == 2)
        def _():
            write_blocks(total_ref[...], block_refs)

    def part_at(n):
        return lax.rem(n + 2, 3)

    field = pl.BlockSpec((None, rows, width), lambda n: (jnp.maximum(n - 1, 0), 0, 0))
    return pl.pallas_call(
        kernel,
        out_shape=[shape((3, rows, width), BF)] + block_shapes(count, tok, model_width),
        grid=(3,),
        in_specs=[
            field,
            pl.BlockSpec((rows, width), lambda n: (0, 0)),
            field,
            pl.BlockSpec((rows, 8), lambda n: (0, 0)),
            pl.BlockSpec((2, width), lambda n: (0, 0)),
            pl.BlockSpec((None, model_width, width), lambda n: (part_at(n), 0, 0)),
        ]
        + [pl.BlockSpec((8, rows), lambda n: (0, 0))] * count,
        out_specs=[pl.BlockSpec((None, rows, width), lambda n: (part_at(n), 0, 0))]
        + [pl.BlockSpec((tok, model_width), lambda n: (0, 0))] * count,
        scratch_shapes=[pltpu.VMEM((rows, model_width), F32)],
        compiler_params=WHOLE,
        cost_estimate=cost(
            6 * rows * model_width * width, 6 * model_width * width + 22 * rows * width + 2 * rows * model_width
        ),
    )(d_norm, d_values, raw, inv, qk_gain, qkv_weight, *sums)


def mlp_forward(hidden_blocks, gate_up_weight, down_weight):
    count = len(hidden_blocks)
    tok, model_width = hidden_blocks[0].shape
    rows = count * tok
    units = down_weight.shape[0]
    tile = min(512, units)
    last = units // tile - 1

    def kernel(*refs):
        gate_w_ref, up_w_ref, down_w_ref, gate_up_ref, swiglu_ref, hidden_ref = refs[
            count : count + 6
        ]
        block_refs = refs[count + 6 : 2 * count + 6]
        total_ref = refs[2 * count + 6]
        step = pl.program_id(0)

        @pl.when(step == 0)
        def _():
            join(refs[:count], hidden_ref)

        gate = dot(hidden_ref[...], gate_w_ref[...])
        up = dot(hidden_ref[...], up_w_ref[...])
        swiglu = (gate * jax.nn.sigmoid(gate) * up).astype(BF)
        gate_up_ref[0] = gate.astype(BF)
        gate_up_ref[1] = up.astype(BF)
        swiglu_ref[...] = swiglu
        product = dot(swiglu, down_w_ref[...])

        @pl.when(step == 0)
        def _():
            total_ref[...] = product

        @pl.when(step > 0)
        def _():
            total_ref[...] += product

        @pl.when(step == last)
        def _():
            write_blocks(total_ref[...], block_refs)

    field = pl.BlockSpec((rows, tile), lambda f: (0, f))
    return pl.pallas_call(
        kernel,
        out_shape=[
            shape((2, rows, units), BF),
            shape((rows, units), BF),
            shape((rows, model_width), BF),
        ]
        + block_shapes(count, tok, model_width),
        grid=(units // tile,),
        in_specs=[pl.BlockSpec((tok, model_width), lambda f: (0, 0))] * count
        + [
            pl.BlockSpec((None, model_width, tile), lambda f: (0, 0, f)),
            pl.BlockSpec((None, model_width, tile), lambda f: (1, 0, f)),
            pl.BlockSpec((tile, model_width), lambda f: (f, 0)),
        ],
        out_specs=[pl.BlockSpec((2, rows, tile), lambda f: (0, 0, f)), field]
        + [pl.BlockSpec((rows, model_width), lambda f: (0, 0))]
        + [pl.BlockSpec((tok, model_width), lambda f: (0, 0))] * count,
        scratch_shapes=[pltpu.VMEM((rows, model_width), F32)],
        compiler_params=WHOLE,
        cost_estimate=cost(
            6 * rows * model_width * units,
            6 * model_width * units + 6 * rows * units + 8 * rows * model_width,
            rows * units,
        ),
    )(*hidden_blocks, gate_up_weight, gate_up_weight, down_weight)


def unit_grads(gate, up, d_swiglu):
    sigmoid = jax.nn.sigmoid(gate)
    d_gate = d_swiglu * up * sigmoid * (1.0 + gate * (1.0 - sigmoid))
    return (d_gate.astype(BF), (d_swiglu * (gate * sigmoid)).astype(BF))


def mlp_back(d_mlp_blocks, gate_up, gate_up_weight, down_weight):
    count = len(d_mlp_blocks)
    tok, model_width = d_mlp_blocks[0].shape
    rows = count * tok
    units = down_weight.shape[0]
    tile = min(512, units)
    last = units // tile - 1

    def kernel(*refs):
        gate_up_ref, gate_w_ref, up_w_ref, down_w_ref, d_gate_up_ref, d_mlp_ref = refs[
            count : count + 6
        ]
        block_refs = refs[count + 6 : 2 * count + 6]
        total_ref = refs[2 * count + 6]
        step = pl.program_id(0)

        @pl.when(step == 0)
        def _():
            join(refs[:count], d_mlp_ref)

        d_swiglu = dot_t(d_mlp_ref[...], down_w_ref[...])
        d_gate, d_up = unit_grads(gate_up_ref[0].astype(F32), gate_up_ref[1].astype(F32), d_swiglu)
        d_gate_up_ref[0] = d_gate
        d_gate_up_ref[1] = d_up
        product = dot_t(d_gate, gate_w_ref[...]) + dot_t(d_up, up_w_ref[...])

        @pl.when(step == 0)
        def _():
            total_ref[...] = product

        @pl.when(step > 0)
        def _():
            total_ref[...] += product

        @pl.when(step == last)
        def _():
            write_blocks(total_ref[...], block_refs)

    field = pl.BlockSpec((2, rows, tile), lambda f: (0, 0, f))
    return pl.pallas_call(
        kernel,
        out_shape=[shape((2, rows, units), BF), shape((rows, model_width), BF)]
        + block_shapes(count, tok, model_width),
        grid=(units // tile,),
        in_specs=[pl.BlockSpec((tok, model_width), lambda f: (0, 0))] * count
        + [
            field,
            pl.BlockSpec((None, model_width, tile), lambda f: (0, 0, f)),
            pl.BlockSpec((None, model_width, tile), lambda f: (1, 0, f)),
            pl.BlockSpec((tile, model_width), lambda f: (f, 0)),
        ],
        out_specs=[field]
        + [pl.BlockSpec((rows, model_width), lambda f: (0, 0))]
        + [pl.BlockSpec((tok, model_width), lambda f: (0, 0))] * count,
        scratch_shapes=[pltpu.VMEM((rows, model_width), F32)],
        compiler_params=WHOLE,
        cost_estimate=cost(
            6 * rows * model_width * units,
            6 * model_width * units + 8 * rows * units + 8 * rows * model_width,
            rows * units,
        ),
    )(*d_mlp_blocks, gate_up, gate_up_weight, gate_up_weight, down_weight)


def mlp_units(hidden, d_mlp_blocks, gate_up_weight, down_weight):
    micro = len(hidden)
    count = len(d_mlp_blocks)
    tok, model_width = d_mlp_blocks[0].shape[1:]
    group = count * tok
    rows = micro * group
    units = down_weight.shape[0]
    tile = min(256, units)

    def kernel(*refs):
        hidden_refs = refs[:micro]
        block_refs = refs[micro : micro + count]
        gate_w_ref, up_w_ref, down_w_ref, d_gate_up_ref, swiglu_ref, d_mlp_ref, rows_ref = refs[
            micro + count :
        ]

        @pl.when(pl.program_id(0) == 0)
        def _():
            for m in range(micro):
                rows_ref[pl.ds(m * group, group), :] = hidden_refs[m][...]
                for j in range(count):
                    d_mlp_ref[pl.ds(m * group + j * tok, tok), :] = block_refs[j][m]

        gate = dot(rows_ref[...], gate_w_ref[...])
        up = dot(rows_ref[...], up_w_ref[...])
        d_gate, d_up = unit_grads(gate, up, dot_t(d_mlp_ref[...], down_w_ref[...]))
        swiglu_ref[...] = (gate * jax.nn.sigmoid(gate) * up).astype(BF)
        d_gate_up_ref[0] = d_gate
        d_gate_up_ref[1] = d_up

    return pl.pallas_call(
        kernel,
        out_shape=[
            shape((2, rows, units), BF),
            shape((rows, units), BF),
            shape((rows, model_width), BF),
        ],
        grid=(units // tile,),
        in_specs=[pl.BlockSpec((group, model_width), lambda f: (0, 0))] * micro
        + [pl.BlockSpec((micro, tok, model_width), lambda f: (0, 0, 0))] * count
        + [
            pl.BlockSpec((None, model_width, tile), lambda f: (0, 0, f)),
            pl.BlockSpec((None, model_width, tile), lambda f: (1, 0, f)),
            pl.BlockSpec((tile, model_width), lambda f: (f, 0)),
        ],
        out_specs=[
            pl.BlockSpec((2, rows, tile), lambda f: (0, 0, f)),
            pl.BlockSpec((rows, tile), lambda f: (0, f)),
            pl.BlockSpec((rows, model_width), lambda f: (0, 0)),
        ],
        scratch_shapes=[pltpu.VMEM((rows, model_width), BF)],
        compiler_params=WHOLE,
        cost_estimate=cost(
            6 * rows * model_width * units,
            6 * rows * model_width + 6 * model_width * units + 6 * rows * units,
            rows * units,
        ),
    )(*hidden, *d_mlp_blocks, gate_up_weight, gate_up_weight, down_weight)


def sum_parts(part_refs):
    total = part_refs[0][...].astype(F32)
    for part_ref in part_refs[1:]:
        total += part_ref[...].astype(F32)
    return total


def norm_back(field, gain, upstream):
    width = field.shape[1]
    inv = lax.rsqrt(jnp.sum(field * field, axis=1, keepdims=True) / width + EPSILON)
    weighted = upstream * gain
    shared = jnp.sum(field * weighted, axis=1, keepdims=True)
    gain_sum = jnp.sum(upstream * field * inv, axis=0, keepdims=True)
    return (inv * weighted - field * (inv * inv * inv * shared / width), gain_sum)


def after_attention(parts, x_rows, post_gain):
    tok, width = x_rows.shape
    count = len(parts)

    def kernel(*refs):
        x_ref, gain_ref, attn_ref, hidden_ref, rounded_ref = refs[count:]
        attn = sum_parts(refs[:count])
        inv = lax.rsqrt(jnp.sum(attn * attn, axis=1, keepdims=True) / width + EPSILON)
        hidden = x_ref[...].astype(F32) + attn * inv * gain_ref[0:1, :]
        attn_ref[...] = attn
        hidden_ref[...] = hidden
        rounded_ref[...] = hidden.astype(BF)

    return pl.pallas_call(
        kernel,
        out_shape=[shape((tok, width), F32), shape((tok, width), F32), shape((tok, width), BF)],
        in_specs=[VMEM] * (count + 2),
        out_specs=[VMEM] * 3,
        cost_estimate=cost(8 * tok * width, 24 * tok * width),
    )(*parts, x_rows, post_gain)


def after_mlp(parts, hidden, grad_rows, post_gain):
    tok, width = hidden.shape
    count = len(parts)

    def kernel(*refs):
        hidden_ref, grad_ref, gain_ref, out_ref, d_mlp_ref, gain_sum_ref = refs[count:]
        mlp = sum_parts(refs[:count])
        gain = gain_ref[1:2, :]
        inv = lax.rsqrt(jnp.sum(mlp * mlp, axis=1, keepdims=True) / width + EPSILON)
        out_ref[...] = hidden_ref[...] + mlp * inv * gain
        d_mlp, gain_sum = norm_back(mlp, gain, grad_ref[...].astype(F32))
        d_mlp_ref[...] = d_mlp.astype(BF)
        gain_sum_ref[...] = gain_sum

    return pl.pallas_call(
        kernel,
        out_shape=[shape((tok, width), F32), shape((tok, width), BF), shape((1, width), F32)],
        in_specs=[VMEM] * (count + 3),
        out_specs=[VMEM] * 3,
        cost_estimate=cost(16 * tok * width, 24 * tok * width),
    )(*parts, hidden, grad_rows, post_gain)


def before_attention(parts, grad_rows, attn, post_gain):
    tok, width = attn.shape
    count = len(parts)

    def kernel(*refs):
        grad_ref, attn_ref, gain_ref, d_hidden_ref, d_attn_ref, gain_sum_ref = refs[count:]
        d_hidden = grad_ref[...].astype(F32) + sum_parts(refs[:count])
        d_hidden_ref[...] = d_hidden
        d_attn, gain_sum = norm_back(attn_ref[...], gain_ref[0:1, :], d_hidden)
        d_attn_ref[...] = d_attn.astype(BF)
        gain_sum_ref[...] = gain_sum

    return pl.pallas_call(
        kernel,
        out_shape=[shape((tok, width), F32), shape((tok, width), BF), shape((1, width), F32)],
        in_specs=[VMEM] * (count + 3),
        out_specs=[VMEM] * 3,
        cost_estimate=cost(16 * tok * width, 24 * tok * width),
    )(*parts, grad_rows, attn, post_gain)


def send_order(top):
    def halves(codes, bit):
        if len(codes) == 1:
            return codes
        return halves([c for c in codes if c & bit], 2 * bit) + halves(
            [c for c in codes if not c & bit], 2 * bit
        )

    stages = []
    bit = 1
    while bit < top:
        stages.append((bit, [bit + c for c in halves(list(range(0, top, 2 * bit)), 2 * bit)]))
        bit *= 2
    return stages


def grad_rows_of(splits, sets):
    codes = [code for split in splits for code in split]
    blocks = len(codes)
    replicas = lax.axis_size("replica")
    order = lax.axis_index("replica") ^ jnp.array(codes, jnp.int32)
    block = sets[0][0].shape[1] // replicas
    planes, _, units = sets[0][1].shape
    tile = min(512, units)
    tiles = units // tile
    width = planes * units
    depth = sum(rows for _, _, _, rows in sets)
    count = len(sets)
    kinds = [BF] * (len(splits) - 1) + [F32]

    def kernel(order_ref, *refs):
        left_refs = refs[: count * blocks]
        right_refs = refs[count * blocks : count * blocks + count]
        out_refs = refs[count * blocks + count : count * blocks + count + len(splits)]
        turned_ref, right_ref = refs[count * blocks + count + len(splits) :]

        @pl.when(pl.program_id(0) == 0)
        def _():
            at = 0
            for k, (_, _, _, rows) in enumerate(sets):
                for b in range(blocks):
                    turned_ref[pl.ds(b * block, block), pl.ds(at, rows)] = left_refs[k * blocks + b][
                        ...
                    ].T
                at += rows

        at = 0
        for k, (_, _, _, rows) in enumerate(sets):
            right_ref[pl.ds(at, rows), :] = right_refs[k][...]
            at += rows
        first = 0
        for split, out_ref in zip(splits, out_refs):
            rows = len(split) * block
            out_ref[...] = dot(turned_ref[pl.ds(first, rows), :], right_ref[...]).astype(out_ref.dtype)
            first += rows

    in_specs = [
        pl.BlockSpec((rows, block), lambda f, order_ref, group=group, b=b: (group, order_ref[b]))
        for _, _, group, rows in sets
        for b in range(blocks)
    ] + [
        pl.BlockSpec(
            (None, rows, tile),
            lambda f, order_ref, group=group: (lax.div(f, tiles), group, lax.rem(f, tiles)),
        )
        for _, _, group, rows in sets
    ]
    return pl.pallas_call(
        kernel,
        out_shape=[shape((len(split) * block, width), kind) for split, kind in zip(splits, kinds)],
        grid_spec=pltpu.PrefetchScalarGridSpec(
            num_scalar_prefetch=1,
            grid=(planes * tiles,),
            in_specs=in_specs,
            out_specs=[
                pl.BlockSpec((len(split) * block, tile), lambda f, order_ref: (0, f))
                for split in splits
            ],
            scratch_shapes=[
                pltpu.VMEM((blocks * block, depth), BF),
                pltpu.VMEM((depth, tile), BF),
            ],
        ),
        compiler_params=WHOLE,
        cost_estimate=cost(
            2 * depth * blocks * block * width,
            2 * depth * (blocks * block + width) + 2 * blocks * block * width,
        ),
    )(
        order,
        *[left for left, _, _, _ in sets for _ in range(blocks)],
        *[right for _, right, _, _ in sets],
    )


def owners_parts(sets, top):
    stages = send_order(top)
    outs = grad_rows_of([codes for _, codes in stages] + [[0]], sets)
    received = []

    def with_adds(codes, out):
        rows = out.shape[0]
        parts = [out]
        for array, held in received:
            first = held.index(codes[0]) // len(codes) * rows
            parts.append(array[first : first + rows])
        return parts

    for (bit, codes), out in zip(stages, outs):
        parts = with_adds(codes, out)
        if len(parts) > 1:
            out = sum(part.astype(F32) for part in parts).astype(BF)
        received.append((exchange(out, "replica", bit), [code ^ bit for code in codes]))
    return (outs[-1], [(array, held.index(0)) for array, held in received])


def finish(parts, planes, turned):
    kept, adds = parts
    rows, width = kept.shape
    units = width // planes
    tile = min(512, units)
    tiles = units // tile

    def kernel(kept_ref, *refs):
        total = kept_ref[...]
        for add_ref in refs[:-1]:
            total += add_ref[...].astype(F32)
        refs[-1][...] = total.T if turned else total

    if turned:
        out_shape = shape((units, rows), F32)
        out_spec = pl.BlockSpec((tile, rows), lambda f: (f, 0))
    else:
        out_shape = shape((planes, rows, units), F32)
        out_spec = pl.BlockSpec(
            (None, rows, tile), lambda f: (lax.div(f, tiles), 0, lax.rem(f, tiles))
        )
    return pl.pallas_call(
        kernel,
        out_shape=out_shape,
        grid=(planes * tiles,),
        in_specs=[pl.BlockSpec((rows, tile), lambda f: (0, f))]
        + [pl.BlockSpec((rows, tile), lambda f, group=group: (group, f)) for _, group in adds],
        out_specs=out_spec,
        compiler_params=WHOLE,
        cost_estimate=cost(rows * width * len(adds), rows * width * (8 + 2 * len(adds))),
    )(kept, *[array for array, _ in adds])


def true_rows(tok_dev):
    size = lax.axis_size("fsdp")
    block = jnp.arange(size, dtype=jnp.int32) ^ lax.axis_index("fsdp")
    return (block[:, None] * tok_dev + jnp.arange(tok_dev, dtype=jnp.int32)[None, :]).reshape(-1)


def tree_tables(parent_row, length_row, places):
    segments = parent_row.shape[0]
    labels = jnp.arange(segments, dtype=jnp.int32)
    before = labels[:, None] >= labels[None, :]
    ends = jnp.sum(jnp.where(before, length_row[None, :], 0), axis=1)
    starts = ends - length_row
    segment_of = jnp.sum((places[:, None] >= ends[None, :]).astype(jnp.int32), axis=1)
    member = segment_of[:, None] == labels[None, :]
    reach = ((labels[:, None] == labels[None, :]) | (parent_row[:, None] == labels[None, :])).astype(F32)
    steps = 1
    while steps < segments - 1:
        reach = (jnp.dot(reach, reach) > 0.5).astype(F32)
        steps *= 2
    ancestry = reach > 0.5
    above = jnp.sum(jnp.where(ancestry, length_row[None, :], 0), axis=1) - length_row
    moved = jnp.sum(jnp.where(member, (above - starts)[None, :], 0), axis=1)
    position = (places + moved).astype(F32)
    member_f = member.astype(F32)
    near = jnp.dot(jnp.dot(member_f, reach), member_f.T) > 0.5
    visible = near & (places[None, :] <= places[:, None])
    freq = ROPE_BASE ** (-jnp.arange(0, HD, 2, dtype=F32) / HD)
    angle = position[:, None] * freq[None, :]
    cos_half, sin_half = jnp.cos(angle), jnp.sin(angle)
    return (
        jnp.where(visible, 0.0, -1e30).astype(F32),
        jnp.concatenate([cos_half, cos_half], axis=1),
        jnp.concatenate([-sin_half, sin_half], axis=1),
    )


def on_device(
    tokens,
    cotangent,
    parents,
    lengths,
    qkv_weight,
    out_weight,
    gate_up_weight,
    down_weight,
    qk_gain,
    post_gain,
):
    micro, tok_dev, model_width = tokens.shape
    local_width = qkv_weight.shape[2]
    size = lax.axis_size("fsdp")
    replicas = lax.axis_size("replica")
    rows = tok_dev * size
    units = down_weight.shape[0]
    micros = range(micro)
    places = true_rows(tok_dev)
    x_blocks = gather_blocks(tokens)
    tables = [tree_tables(parents[m, 0], lengths[m, 0], places) for m in micros]

    projected = [project([block[m] for block in x_blocks], qkv_weight) for m in micros]
    attended = []
    for m in micros:
        raw, values, squares, _ = projected[m]
        attended.append(
            attend(raw, values, gather_blocks(squares), *tables[m], qk_gain, out_weight)
        )
    residual = []
    for m in micros:
        parts = swap_blocks(attended[m][4:])
        residual.append(after_attention(parts, tokens[m], post_gain))
    expanded = [
        mlp_forward(gather_blocks(residual[m][2]), gate_up_weight, down_weight) for m in micros
    ]
    far = replicas // 2
    far_hidden = [exchange(expanded[m][2], "replica", far) for m in micros]
    finals = []
    for m in micros:
        parts = swap_blocks(expanded[m][3:])
        finals.append(after_mlp(parts, residual[m][1], cotangent[m], post_gain))
    shrunk = [
        mlp_back(gather_blocks(finals[m][1]), expanded[m][0], gate_up_weight, down_weight)
        for m in micros
    ]
    far_d_mlp = gather_blocks(exchange(jnp.stack([final[1] for final in finals]), "replica", far))
    far_d_gate_up, far_swiglu, far_d_mlp = mlp_units(
        far_hidden, far_d_mlp, gate_up_weight, down_weight
    )
    down_parts = owners_parts(
        [(shrunk[m][1], expanded[m][1][None], 0, rows) for m in micros]
        + [(far_d_mlp, far_swiglu[None], 0, micro * rows)],
        far,
    )
    gate_up_parts = owners_parts(
        [(expanded[m][2], shrunk[m][0], 0, rows) for m in micros]
        + [(jnp.concatenate(far_hidden, axis=0), far_d_gate_up, 0, micro * rows)],
        far,
    )
    entering = []
    for m in micros:
        parts = swap_blocks(shrunk[m][2:])
        entering.append(before_attention(parts, cotangent[m], residual[m][0], post_gain))
    unattended = []
    for m in micros:
        raw, values = projected[m][:2]
        _, queries, keys, inv = attended[m][:4]
        unattended.append(
            attend_back(
                gather_blocks(entering[m][1]),
                out_weight,
                queries,
                keys,
                values,
                raw,
                inv,
                *tables[m],
                qk_gain,
            )
        )
    out_parts = owners_parts(
        [(unattended[m][0], attended[m][0][None], 0, rows) for m in micros], replicas
    )
    unprojected = []
    for m in micros:
        _, d_norm, d_values, sums, _ = unattended[m]
        unprojected.append(
            project_back(
                d_norm,
                d_values,
                projected[m][0],
                attended[m][3],
                gather_blocks(sums),
                qk_gain,
                qkv_weight,
            )
        )
    qkv_parts = owners_parts(
        [(projected[m][3], unprojected[m][0], 0, rows) for m in micros], replicas
    )
    input_grads = []
    for m in micros:
        parts = swap_blocks(unprojected[m][1:])
        input_grads.append(entering[m][0] + sum(part.astype(F32) for part in parts))

    query_key_rows = sum(unattended[m][4] for m in micros)
    gain_rows = jnp.concatenate(
        [sum(entering[m][2] for m in micros), sum(finals[m][2] for m in micros)], axis=0
    )
    me = lax.axis_index("fsdp")
    split = gain_rows.reshape(2, size, local_width)
    post_rows = lax.dynamic_index_in_dim(split, me, 1, keepdims=False)
    for flip in range(1, size):
        sent = lax.dynamic_index_in_dim(split, me ^ flip, 1, keepdims=False)
        post_rows = post_rows + exchange(sent, "fsdp", flip)
    sums = sum_small(jnp.concatenate([query_key_rows, post_rows], axis=0), "replica")
    return (
        jnp.stack([final[0] for final in finals]),
        jnp.stack(input_grads),
        finish(qkv_parts, 3, False),
        finish(out_parts, 1, True),
        finish(gate_up_parts, 2, False),
        finish(down_parts, 1, True),
        sums[:2],
        sums[2:],
    )


def solution(mesh):
    in_specs = (
        P(None, ("replica", "fsdp"), None),
        P(None, ("replica", "fsdp"), None),
        P(None, "replica", None),
        P(None, "replica", None),
        P(None, None, "fsdp"),
        P("fsdp", None),
        P(None, None, "fsdp"),
        P("fsdp", None),
        P(None, "fsdp"),
        P(),
    )
    out_specs = (
        P(None, ("replica", "fsdp"), None),
        P(None, ("replica", "fsdp"), None),
        P(None, "replica", "fsdp"),
        P("fsdp", "replica"),
        P(None, "replica", "fsdp"),
        P("fsdp", "replica"),
        P(None, "fsdp"),
        P(None, "fsdp"),
    )
    return jax.shard_map(
        on_device, mesh=mesh, in_specs=in_specs, out_specs=out_specs, check_vma=False
    )
```

time: 696 us -> 557 us (0.80)
  Pallas kernels: 0 us -> 209 us
  waiting for transfers between devices: 345 us -> 194 us
  matrix products: 127 us -> 3.4 us
  local copies, waits for them, and re-layouts: 77.3 us -> 17.6 us
  starting transfers between devices: 82.5 us -> 101 us
  other arithmetic: 37.8 us -> 20.6 us
  between operations: 16.4 us -> 1.53 us
    reduce_scatter x4 -> x0, waiting for transfers between devices: 261 us -> none  [to_owners(): lax.psum_scatter(grad, 'replica', scatter_dimension=dim, tiled=True)]
    pallas_call x0 -> x27, Pallas kernels: none -> 209 us  [the longest x4 37.3 us: grad_rows_of(): pl.pallas_call(kernel, out_shape=[shape((len(split) * block, width), kind...]
    dot_general x38 -> x6, matrix products: 127 us -> 3.4 us  [the longest x2 2.11 us: tree_tables(): near = jnp.dot(jnp.dot(member_f, reach), member_f.T) > 0.5]
    ppermute x66 -> x79, waiting for transfers between devices: 83.9 us -> 194 us  [exchange(): return lax.ppermute(value, axis, [(i, i ^ flip) for i in range(size)])]
    unnamed x312 -> x156, local copies, waits for them, and re-layouts: 33.6 us -> 11.4 us
    ppermute x66 -> x79, starting transfers between devices: 82.1 us -> 101 us  [exchange(): return lax.ppermute(value, axis, [(i, i ^ flip) for i in range(size)])]
    reshape x18 -> x0, local copies, waits for them, and re-layouts: 16.3 us -> none  [the longest x12 6.2 us: sum_row_values(): blocks = exchange(value, 'fsdp', flip).reshape(kinds, size, rows // size)]
    reduce_sum x14 -> x2, other arithmetic: 10.1 us -> 0.18 us  [the longest x1 0.09 us: tree_tables(): jnp.sum((places[:, None] >= ends[None, :]).astype(jnp.int32), axis=1)]
  transfers between devices with their start and end apart: 70 -> 79, of which waited for: 29 -> 23; matrix products, arithmetic and copies ran while one was open for 28% -> 5% of each run, Pallas kernels for 0% -> 35%
where the time goes in v3:
time: 557 us; the launch traced here: 547 us
  Pallas kernels  209 us (38%)
  waiting for transfers between devices  194 us (35%)
  starting transfers between devices  101 us (18%)
  other arithmetic  20.6 us (4%)
  local copies, waits for them, and re-layouts  17.6 us (3%)
    ppermute x79, waiting for transfers between devices, exchange(): return lax.ppermute(value, axis, [(i, i ^ flip) for i in range(size)])  194 us
    ppermute x79, starting transfers between devices, exchange(): return lax.ppermute(value, axis, [(i, i ^ flip) for i in range(size)])  101 us
    pallas_call x4, Pallas kernels, grad_rows_of(): pl.pallas_call(kernel, out_shape=[shape((len(split) * block, width), kind...  37.3 us
    pallas_call x2, Pallas kernels, mlp_back(): pl.pallas_call(kernel, out_shape=[shape((2, rows, units), BF), shape((row...  31.6 us
    pallas_call x2, Pallas kernels, mlp_forward(): pl.pallas_call(kernel, out_shape=[shape((2, rows, units), BF), shape((row...  30.6 us
    pallas_call x1, Pallas kernels, mlp_units(): pl.pallas_call(kernel, out_shape=[shape((2, rows, units), BF), shape((row...  20.7 us
    pallas_call x4, Pallas kernels, finish(): pl.pallas_call(kernel, out_shape=out_shape, grid=(planes * tiles,), in_sp...  18.4 us
    pallas_call x2, Pallas kernels, project_back(): pl.pallas_call(kernel, out_shape=[shape((3, rows, width), BF)] + block_sh...  15 us
  transfers between devices with their start and end apart: 79, of which 23 were waited for; matrix products, arithmetic and copies ran while one was open for 5% of the time, Pallas kernels for 35%

profile of v3, /device:TPU:0, one launch (start us, length us, event | category | flops | bytes accessed | tf_op | source)
XLA Modules:
  0.0 546.8 jit_solution(7869498712064814694)
XLA Ops:
  17.5 11.0 %collective-permute-done.1 = bf16[2,64,2048]{2,1,0:T(8,128)(2,1)S(1)} collective-permute-done((bf16[2,64,2048]{2,1,0:T(8,128)(2,1)}, bf16[2,64,2048]{2,1,0:T(8,128)(2,1)S(1)}, u32[]{:S(2)}, u32[]{:S(2)}) %collective-permute-start.1) | collective-permute-done | bytes 524320 | tf_op jit(solution)/shard_map/ppermute | solution.py:19
  30.2 7.1 %shard_map.197 = (f32[2,256,512]{2,1,0:T(8,128)}, bf16[256,512]{1,0:T(8,128)(2,1)}, f32[8,256]{1,0:T(8,128)}, bf16[256,2048]{1,0:T(8,128)(2,1)}) custom-call(bf16[64,2048]{1,0:T(8,128)(2,1)} %get-tuple-element.232.refs_0_.refs_4_, bf16[64,2048]{1,0:T(8,128)(2,1)} %get-tuple-element.230.refs_1_, bf16[64,2048]{1,0:T(8,128)(2,1)} %get-tuple-element.228.refs_2_, ...), custom_call_target="tpu_custom_call" | custom-call | flops 1610612736 | bytes 7340032 | tf_op jit(solution)/shard_map/pallas_call | solution.py:139
  40.8 6.9 %shard_map.202 = (f32[2,256,512]{2,1,0:T(8,128)}, bf16[256,512]{1,0:T(8,128)(2,1)}, f32[8,256]{1,0:T(8,128)}, bf16[256,2048]{1,0:T(8,128)(2,1)}) custom-call(bf16[64,2048]{1,0:T(8,128)(2,1)} %get-tuple-element.233.refs_0_.refs_4_, bf16[64,2048]{1,0:T(8,128)(2,1)} %get-tuple-element.231.refs_1_, bf16[64,2048]{1,0:T(8,128)(2,1)} %get-tuple-element.229.refs_2_, ...), custom_call_target="tpu_custom_call" | custom-call | flops 1610612736 | bytes 7340032 | tf_op jit(solution)/shard_map/pallas_call | solution.py:139
  51.8 5.6 %shard_map.198 = (bf16[256,512]{1,0:T(8,128)(2,1)}, bf16[256,512]{1,0:T(8,128)(2,1)}, bf16[256,512]{1,0:T(8,128)(2,1)}, f32[256,8]{1,0:T(8,128)}, f32[64,2048]{1...) custom-call(f32[2,256,512]{2,1,0:T(8,128)} %get-tuple-element.113.raw_ref.refs_8_, ...), custom_call_target="tpu_custom_call" | custom-call | flops 671088640 | bytes 4980736 | tf_op jit(solution)/shard_map/pallas_call | solution.py:188
  77.4 8.7 %collective-permute-done.19.refs_2_ = bf16[64,2048]{1,0:T(8,128)(2,1)S(1)} collective-permute-done((bf16[64,2048]{1,0:T(8,128)(2,1)}, bf16[64,2048]{1,0:T(8,128)(2,1)S(1)}, u32[]{:S(2)}, u32[]{:S(2)}) %collective-permute-start.19) | collective-permute-done | bytes 262176 | tf_op jit(solution)/shard_map/ppermute | solution.py:19
  97.3 15.1 %shard_map.200 = (bf16[2,256,2048]{2,1,0:T(8,128)(2,1)}, bf16[256,2048]{1,0:T(8,128)(2,1)}, bf16[256,2048]{1,0:T(8,128)(2,1)}, f32[64,2048]{1,0:T(8,128)}, bf16[...) custom-call(bf16[64,2048]{1,0:T(8,128)(2,1)} %get-tuple-element.120.refs_0_, ...), custom_call_target="tpu_custom_call" | custom-call | flops 6442450944 | bytes 32505856 | tf_op jit(solution)/shard_map/pallas_call | solution.py:402
  120.3 15.5 %shard_map.205 = (bf16[2,256,2048]{2,1,0:T(8,128)(2,1)}, bf16[256,2048]{1,0:T(8,128)(2,1)}, bf16[256,2048]{1,0:T(8,128)(2,1)}, f32[64,2048]{1,0:T(8,128)}, bf16[...) custom-call(bf16[64,2048]{1,0:T(8,128)(2,1)} %get-tuple-element.134.refs_0_, ...), custom_call_target="tpu_custom_call" | custom-call | flops 6442450944 | bytes 32505856 | tf_op jit(solution)/shard_map/pallas_call | solution.py:402
  147.3 8.7 %collective-permute-done.25.refs_2_ = bf16[64,2048]{1,0:T(8,128)(2,1)S(1)} collective-permute-done((bf16[64,2048]{1,0:T(8,128)(2,1)}, bf16[64,2048]{1,0:T(8,128)(2,1)S(1)}, u32[]{:S(2)}, u32[]{:S(2)}) %collective-permute-start.25) | collective-permute-done | bytes 262176 | tf_op jit(solution)/shard_map/ppermute | solution.py:19
  167.5 15.8 %shard_map.207 = (bf16[2,256,2048]{2,1,0:T(8,128)(2,1)}, bf16[256,2048]{1,0:T(8,128)(2,1)}, f32[64,2048]{1,0:T(8,128)}, bf16[64,2048]{1,0:T(8,128)(2,1)}, bf16[6...) custom-call(bf16[64,2048]{1,0:T(8,128)(2,1)} %get-tuple-element.141.refs_0_, bf16[64,2048]{1,0:T(8,128)(2,1)} %copy-done.26, ...), custom_call_target="tpu_custom_call" | custom-call | flops 6442450944 | bytes 33554432 | tf_op jit(solution)/shard_map/pallas_call | solution.py:475
  187.6 15.7 %shard_map.211 = (bf16[2,256,2048]{2,1,0:T(8,128)(2,1)}, bf16[256,2048]{1,0:T(8,128)(2,1)}, f32[64,2048]{1,0:T(8,128)}, bf16[64,2048]{1,0:T(8,128)(2,1)}, bf16[6...) custom-call(bf16[64,2048]{1,0:T(8,128)(2,1)} %get-tuple-element.160.refs_0_, bf16[64,2048]{1,0:T(8,128)(2,1)} %copy-done.27, ...), custom_call_target="tpu_custom_call" | custom-call | flops 6442450944 | bytes 33554432 | tf_op jit(solution)/shard_map/pallas_call | solution.py:475
  242.3 6.8 %shard_map.209 = (bf16[256,2048]{1,0:T(8,128)(2,1)}, f32[2,256,512]{2,1,0:T(8,128)}, bf16[256,512]{1,0:T(8,128)(2,1)}, f32[8,256]{1,0:T(8,128)}, f32[2,512]{1,0:T(2,128)}) custom-call(bf16[64,2048]{1,0:T(8,128)(2,1)} %get-tuple-element.149.refs_0_, bf16[64,2048]{1,0:T(8,128)(2,1)} %copy-done.32, bf16[64,2048]{1,0:T(8,128)(2,1)} %copy-done.31, ...), custom_call_target="tpu_custom_call" | custom-call | flops 872415232 | bytes 6291456 | tf_op jit(solution)/shard_map/pallas_call | solution.py:260
  249.2 10.7 %collective-permute-done.63.refs_0_ = bf16[256,2048]{1,0:T(8,128)(2,1)S(1)} collective-permute-done((bf16[256,2048]{1,0:T(8,128)(2,1)}, bf16[256,2048]{1,0:T(8,128)(2,1)S(1)}, u32[]{:S(2)}, u32[]{:S(2)}) %collective-permute-start.63) | collective-permute-done | bytes 1048608 | tf_op jit(solution)/shard_map/ppermute | solution.py:19
  261.6 6.9 %shard_map.213 = (bf16[256,2048]{1,0:T(8,128)(2,1)}, f32[2,256,512]{2,1,0:T(8,128)}, bf16[256,512]{1,0:T(8,128)(2,1)}, f32[8,256]{1,0:T(8,128)}, f32[2,512]{1,0:T(2,128)}) custom-call(bf16[64,2048]{1,0:T(8,128)(2,1)} %get-tuple-element.168.refs_0_, bf16[64,2048]{1,0:T(8,128)(2,1)} %collective-permute-done.48.refs_1_, bf16[64,2048]{1,0:T(8,128)(2,1)} %copy-done.34, ...), custom_call_target="tpu_custom_call" | custom-call | flops 872415232 | bytes 6291456 | tf_op jit(solution)/shard_map/pallas_call | solution.py:260
  268.5 12.8 %collective-permute-done.64.refs_1_ = bf16[256,2048]{1,0:T(8,128)(2,1)S(1)} collective-permute-done((bf16[256,2048]{1,0:T(8,128)(2,1)}, bf16[256,2048]{1,0:T(8,128)(2,1)S(1)}, u32[]{:S(2)}, u32[]{:S(2)}) %collective-permute-start.64) | collective-permute-done | bytes 1048608 | tf_op jit(solution)/shard_map/ppermute | solution.py:19
  288.0 7.6 %shard_map.210 = (bf16[3,256,512]{2,1,0:T(8,128)(2,1)}, f32[64,2048]{1,0:T(8,128)}, bf16[64,2048]{1,0:T(8,128)(2,1)}, bf16[64,2048]{1,0:T(8,128)(2,1)}, bf16[64,2048]{1,0:T(8,128)(2,1)}) custom-call(f32[2,256,512]{2,1,0:T(8,128)} %get-tuple-element.153.d_norm_ref, bf16[256,512]{1,0:T(8,128)(2,1)} %get-tuple-element.154.d_values_ref, ...), custom_call_target="tpu_custom_call" | custom-call | flops 1610612736 | bytes 10223616 | tf_op jit(solution)/shard_map/pallas_call | solution.py:338
  296.3 20.7 %shard_map.219 = (bf16[2,512,2048]{2,1,0:T(8,128)(2,1)}, bf16[512,2048]{1,0:T(8,128)(2,1)}, bf16[512,2048]{1,0:T(8,128)(2,1)}) custom-call(bf16[256,2048]{1,0:T(8,128)(2,1)} %copy-done.9, bf16[256,2048]{1,0:T(8,128)(2,1)} %copy-done.10, bf16[2,64,2048]{2,1,0:T(8,128)(2,1)} %collective-permute-done.65.refs_2_, ...), custom_call_target="tpu_custom_call" | custom-call | flops 12884901888 | bytes 37748736 | tf_op jit(solution)/shard_map/pallas_call | solution.py:530
  317.0 15.0 %shard_map.220 = (bf16[512,4096]{1,0:T(8,128)(2,1)}, bf16[256,4096]{1,0:T(8,128)(2,1)}, f32[256,4096]{1,0:T(8,128)}) custom-call(s32[4]{0:T(128)} %broadcast_xor_fusion.order_ref, bf16[256,2048]{1,0:T(8,128)(2,1)} %get-tuple-element.195.refs_0_.refs_1_.refs_2_.refs_3_, bf16[256,2048]{1,0:T(8,128)(2,1)} %get-tuple-element.195.refs_0_.refs_1_.refs_2_.refs_3_, ...), custom_call_target="tpu_custom_call" | custom-call | flops 8589934592 | bytes 18874368 | tf_op jit(solution)/shard_map/pallas_call | solution.py:709
  332.7 7.5 %shard_map.214 = (bf16[3,256,512]{2,1,0:T(8,128)(2,1)}, f32[64,2048]{1,0:T(8,128)}, bf16[64,2048]{1,0:T(8,128)(2,1)}, bf16[64,2048]{1,0:T(8,128)(2,1)}, bf16[64,2048]{1,0:T(8,128)(2,1)}) custom-call(f32[2,256,512]{2,1,0:T(8,128)} %get-tuple-element.172.d_norm_ref, bf16[256,512]{1,0:T(8,128)(2,1)} %get-tuple-element.173.d_values_ref, ...), custom_call_target="tpu_custom_call" | custom-call | flops 1610612736 | bytes 10223616 | tf_op jit(solution)/shard_map/pallas_call | solution.py:338
  340.3 8.2 %shard_map.215 = (bf16[1024,1536]{1,0:T(8,128)(2,1)}, bf16[512,1536]{1,0:T(8,128)(2,1)}, bf16[256,1536]{1,0:T(8,128)(2,1)}, f32[256,1536]{1,0:T(8,128)}) custom-call(s32[8]{0:T(128)} %broadcast_xor_fusion.1.order_ref, bf16[256,2048]{1,0:T(8,128)(2,1)} %get-tuple-element.179.refs_0_.refs_1_.refs_2_.refs_3_.refs_4_.refs_5_.refs_6_.refs_7_, ...), custom_call_target="tpu_custom_call" | custom-call | flops 3221225472 | bytes 9961472 | tf_op jit(solution)/shard_map/pallas_call | solution.py:709
  371.8 9.5 %shard_map.222 = (bf16[512,2048]{1,0:T(8,128)(2,1)}, bf16[256,2048]{1,0:T(8,128)(2,1)}, f32[256,2048]{1,0:T(8,128)}) custom-call(s32[4]{0:T(128)} %broadcast_xor_fusion.order_ref, bf16[256,2048]{1,0:T(8,128)(2,1)} %get-tuple-element.203.refs_0_.refs_1_.refs_2_.refs_3_, bf16[256,2048]{1,0:T(8,128)(2,1)} %get-tuple-element.203.refs_0_.refs_1_.refs_2_.refs_3_, ...), custom_call_target="tpu_custom_call" | custom-call | flops 4294967296 | bytes 10485760 | tf_op jit(solution)/shard_map/pallas_call | solution.py:709
  396.2 26.9 %collective-permute-done.58.refs_1_ = bf16[512,1536]{1,0:T(8,128)(2,1)S(1)} collective-permute-done((bf16[512,1536]{1,0:T(8,128)(2,1)S(1)}, bf16[512,1536]{1,0:T(8,128)(2,1)S(1)}, u32[]{:S(2)}, u32[]{:S(2)}) %collective-permute-start.58) | collective-permute-done | bytes 1572896 | tf_op jit(solution)/shard_map/ppermute | solution.py:19
  425.5 53.8 %collective-permute-done.61.refs_1_ = bf16[512,512]{1,0:T(8,128)(2,1)S(1)} collective-permute-done((bf16[512,512]{1,0:T(8,128)(2,1)S(1)}, bf16[512,512]{1,0:T(8,128)(2,1)S(1)}, u32[]{:S(2)}, u32[]{:S(2)}) %collective-permute-start.61) | collective-permute-done | bytes 524320 | tf_op jit(solution)/shard_map/ppermute | solution.py:19
  483.6 43.0 %collective-permute-done.62.refs_2_ = bf16[256,512]{1,0:T(8,128)(2,1)S(1)} collective-permute-done((bf16[256,512]{1,0:T(8,128)(2,1)S(1)}, bf16[256,512]{1,0:T(8,128)(2,1)S(1)}, u32[]{:S(2)}, u32[]{:S(2)}) %collective-permute-start.62) | collective-permute-done | bytes 262176 | tf_op jit(solution)/shard_map/ppermute | solution.py:19
  539.0 7.7 %shard_map.221 = f32[2,256,2048]{2,1,0:T(8,128)} custom-call(f32[256,4096]{1,0:T(8,128)} %get-tuple-element.200.kept_ref, bf16[512,4096]{1,0:T(8,128)(2,1)} %collective-permute-done.69.refs_0_, bf16[256,4096]{1,0:T(8,128)(2,1)} %collective-permute-done.70.refs_1_), custom_call_target="tpu_custom_call" | custom-call | flops 2097152 | bytes 12582912 | tf_op jit(solution)/shard_map/pallas_call | solution.py:779
  (368 shorter events, 198.1 us)
Async XLA Ops:
  3.7 24.8 %collective-permute-start.1 = (bf16[2,64,2048]{2,1,0:T(8,128)(2,1)}, bf16[2,64,2048]{2,1,0:T(8,128)(2,1)S(1)}, u32[]{:S(2)}, u32[]{:S(2)}) collective-permute-start(bf16[2,64,2048]{2,1,0:T(8,128)(2,1)} %param.14), channel_id=1, source_target_pairs={{0,2},{1,3},{2,0},{3,1},{4,6},{5,7},{6,4},{7,5},{8,10},{9,11},{10,... | collective-permute-start | bytes 1572872 | tf_op jit(solution)/shard_map/ppermute | solution.py:19
  89.5 29.2 %collective-permute-start.23 = (bf16[64,2048]{1,0:T(8,128)(2,1)}, bf16[64,2048]{1,0:T(8,128)(2,1)S(1)}, u32[]{:S(2)}, u32[]{:S(2)}) collective-permute-start(bf16[64,2048]{1,0:T(8,128)(2,1)} %get-tuple-element.134.refs_0_), channel_id=1, source_target_pairs={{0,3},{1,2},{2,1},{3,0},{4,7},{5,6},{6,5},{7,4},{8,11},{9,10},{10,... | collective-permute-start | bytes 786440 | tf_op jit(solution)/shard_map/ppermute | solution.py:19
  112.4 26.9 %collective-permute-start.12 = (bf16[64,2048]{1,0:T(8,128)(2,1)}, bf16[64,2048]{1,0:T(8,128)(2,1)S(1)}, u32[]{:S(2)}, u32[]{:S(2)}) collective-permute-start(bf16[64,2048]{1,0:T(8,128)(2,1)} %get-tuple-element.122), channel_id=1, source_target_pairs={{0,1},{1,0},{2,3},{3,2},{4,5},{5,4},{6,7},{7,6},{8,9},{9,8},{10,11... | collective-permute-start | bytes 786440 | tf_op jit(solution)/shard_map/ppermute | solution.py:19
  114.0 26.2 %collective-permute-start.13 = (bf16[64,2048]{1,0:T(8,128)(2,1)}, bf16[64,2048]{1,0:T(8,128)(2,1)S(1)}, u32[]{:S(2)}, u32[]{:S(2)}) collective-permute-start(bf16[64,2048]{1,0:T(8,128)(2,1)} %get-tuple-element.123), channel_id=1, source_target_pairs={{0,2},{1,3},{2,0},{3,1},{4,6},{5,7},{6,4},{7,5},{8,10},{9,11},{10,... | collective-permute-start | bytes 786440 | tf_op jit(solution)/shard_map/ppermute | solution.py:19
  159.6 25.4 %collective-permute-start.43 = (bf16[64,2048]{1,0:T(8,128)(2,1)}, bf16[64,2048]{1,0:T(8,128)(2,1)S(1)}, u32[]{:S(2)}, u32[]{:S(2)}) collective-permute-start(bf16[64,2048]{1,0:T(8,128)(2,1)} %get-tuple-element.160.refs_0_), channel_id=1, source_target_pairs={{0,2},{1,3},{2,0},{3,1},{4,6},{5,7},{6,4},{7,5},{8,10},{9,11},{10,... | collective-permute-start | bytes 786440 | tf_op jit(solution)/shard_map/ppermute | solution.py:19
  164.2 43.1 %collective-permute-start.65 = (bf16[2,64,2048]{2,1,0:T(8,128)(2,1)S(1)}, bf16[2,64,2048]{2,1,0:T(8,128)(2,1)}, u32[]{:S(2)}, u32[]{:S(2)}) collective-permute-start(bf16[2,64,2048]{2,1,0:T(8,128)(2,1)S(1)} %pad_maximum_fusion.3), channel_id=1, source_target_pairs={{0,16},{4,20},{8,24},{12,28},{16,0},{20,4},{24,8},{28,12},{1,17},{... | collective-permute-start | bytes 1572872 | tf_op jit(solution)/shard_map/ppermute | solution.py:19
  206.9 52.9 %collective-permute-start.63 = (bf16[256,2048]{1,0:T(8,128)(2,1)}, bf16[256,2048]{1,0:T(8,128)(2,1)S(1)}, u32[]{:S(2)}, u32[]{:S(2)}) collective-permute-start(bf16[256,2048]{1,0:T(8,128)(2,1)} %get-tuple-element.195.refs_0_.refs_1_.refs_2_.refs_3_), channel_id=1, source_target_pairs={{0,16},{4,20},{8,24},{12,28},{16,0},{20,4},{24,8},{28,12},{1,17},{... | collective-permute-start | bytes 3145736 | tf_op jit(solution)/shard_map/ppermute | solution.py:19
  207.2 74.0 %collective-permute-start.64 = (bf16[256,2048]{1,0:T(8,128)(2,1)}, bf16[256,2048]{1,0:T(8,128)(2,1)S(1)}, u32[]{:S(2)}, u32[]{:S(2)}) collective-permute-start(bf16[256,2048]{1,0:T(8,128)(2,1)} %get-tuple-element.196.refs_4_.refs_5_.refs_6_.refs_7_), channel_id=1, source_target_pairs={{0,16},{4,20},{8,24},{12,28},{16,0},{20,4},{24,8},{28,12},{1,17},{... | collective-permute-start | bytes 3145736 | tf_op jit(solution)/shard_map/ppermute | solution.py:19
  234.2 61.4 %collective-permute-start.68 = (bf16[2,64,2048]{2,1,0:T(8,128)(2,1)}, bf16[2,64,2048]{2,1,0:T(8,128)(2,1)}, u32[]{:S(2)}, u32[]{:S(2)}) collective-permute-start(bf16[2,64,2048]{2,1,0:T(8,128)(2,1)} %collective-permute-done.65.refs_2_), channel_id=1, source_target_pairs={{0,3},{1,2},{2,1},{3,0},{4,7},{5,6},{6,5},{7,4},{8,11},{9,10},{10,... | collective-permute-start | bytes 1572872 | tf_op jit(solution)/shard_map/ppermute | solution.py:19
  239.1 57.2 %collective-permute-start.67 = (bf16[2,64,2048]{2,1,0:T(8,128)(2,1)}, bf16[2,64,2048]{2,1,0:T(8,128)(2,1)}, u32[]{:S(2)}, u32[]{:S(2)}) collective-permute-start(bf16[2,64,2048]{2,1,0:T(8,128)(2,1)} %collective-permute-done.65.refs_2_), channel_id=1, source_target_pairs={{0,2},{1,3},{2,0},{3,1},{4,6},{5,7},{6,4},{7,5},{8,10},{9,11},{10,... | collective-permute-start | bytes 1572872 | tf_op jit(solution)/shard_map/ppermute | solution.py:19
  240.7 55.6 %collective-permute-start.66 = (bf16[2,64,2048]{2,1,0:T(8,128)(2,1)}, bf16[2,64,2048]{2,1,0:T(8,128)(2,1)}, u32[]{:S(2)}, u32[]{:S(2)}) collective-permute-start(bf16[2,64,2048]{2,1,0:T(8,128)(2,1)} %collective-permute-done.65.refs_2_), channel_id=1, source_target_pairs={{0,1},{1,0},{2,3},{3,2},{4,5},{5,4},{6,7},{7,6},{8,9},{9,8},{10,11... | collective-permute-start | bytes 1572872 | tf_op jit(solution)/shard_map/ppermute | solution.py:19
  285.1 47.0 %collective-permute-start.53 = (f32[8,256]{1,0:T(8,128)S(1)}, f32[8,256]{1,0:T(8,128)S(1)}, u32[]{:S(2)}, u32[]{:S(2)}) collective-permute-start(f32[8,256]{1,0:T(8,128)S(1)} %copy-done.64), channel_id=1, source_target_pairs={{0,3},{1,2},{2,1},{3,0},{4,7},{5,6},{6,5},{7,4},{8,11},{9,10},{10,... | collective-permute-start | bytes 24584 | tf_op jit(solution)/shard_map/ppermute | solution.py:19
  286.7 45.4 %collective-permute-start.52 = (f32[8,256]{1,0:T(8,128)S(1)}, f32[8,256]{1,0:T(8,128)S(1)}, u32[]{:S(2)}, u32[]{:S(2)}) collective-permute-start(f32[8,256]{1,0:T(8,128)S(1)} %copy-done.64), channel_id=1, source_target_pairs={{0,2},{1,3},{2,0},{3,1},{4,6},{5,7},{6,4},{7,5},{8,10},{9,11},{10,... | collective-permute-start | bytes 24584 | tf_op jit(solution)/shard_map/ppermute | solution.py:19
  295.6 36.5 %collective-permute-start.51 = (f32[8,256]{1,0:T(8,128)S(1)}, f32[8,256]{1,0:T(8,128)S(1)}, u32[]{:S(2)}, u32[]{:S(2)}) collective-permute-start(f32[8,256]{1,0:T(8,128)S(1)} %copy-done.64), channel_id=1, source_target_pairs={{0,1},{1,0},{2,3},{3,2},{4,5},{5,4},{6,7},{7,6},{8,9},{9,8},{10,11... | collective-permute-start | bytes 24584 | tf_op jit(solution)/shard_map/ppermute | solution.py:19
  332.0 53.7 %collective-permute-start.69 = (bf16[512,4096]{1,0:T(8,128)(2,1)}, bf16[512,4096]{1,0:T(8,128)(2,1)}, u32[]{:S(2)}, u32[]{:S(2)}) collective-permute-start(bf16[512,4096]{1,0:T(8,128)(2,1)} %get-tuple-element.201), channel_id=1, source_target_pairs={{0,4},{4,0},{8,12},{12,8},{16,20},{20,16},{24,28},{28,24},{1,5},{5... | collective-permute-start | bytes 12582920 | tf_op jit(solution)/shard_map/ppermute | solution.py:19
  348.4 36.3 %collective-permute-start.57 = (bf16[1024,1536]{1,0:T(8,128)(2,1)}, bf16[1024,1536]{1,0:T(8,128)(2,1)S(1)}, u32[]{:S(2)}, u32[]{:S(2)}) collective-permute-start(bf16[1024,1536]{1,0:T(8,128)(2,1)} %get-tuple-element.184), channel_id=1, source_target_pairs={{0,4},{4,0},{8,12},{12,8},{16,20},{20,16},{24,28},{28,24},{1,5},{5... | collective-permute-start | bytes 9437192 | tf_op jit(solution)/shard_map/ppermute | solution.py:19
  384.8 95.1 %collective-permute-start.55 = (bf16[64,2048]{1,0:T(8,128)(2,1)S(1)}, bf16[64,2048]{1,0:T(8,128)(2,1)S(1)}, u32[]{:S(2)}, u32[]{:S(2)}) collective-permute-start(bf16[64,2048]{1,0:T(8,128)(2,1)S(1)} %copy-done.75), channel_id=1, source_target_pairs={{0,2},{1,3},{2,0},{3,1},{4,6},{5,7},{6,4},{7,5},{8,10},{9,11},{10,... | collective-permute-start | bytes 786440 | tf_op jit(solution)/shard_map/ppermute | solution.py:19
  385.8 37.3 %collective-permute-start.58 = (bf16[512,1536]{1,0:T(8,128)(2,1)S(1)}, bf16[512,1536]{1,0:T(8,128)(2,1)S(1)}, u32[]{:S(2)}, u32[]{:S(2)}) collective-permute-start(bf16[512,1536]{1,0:T(8,128)(2,1)S(1)} %add_convert_fusion.1), channel_id=1, source_target_pairs={{0,8},{4,12},{8,0},{12,4},{16,24},{20,28},{24,16},{28,20},{1,9},{5... | collective-permute-start | bytes 4718600 | tf_op jit(solution)/shard_map/ppermute | solution.py:19
  391.2 147.8 %collective-permute-start.70 = (bf16[256,4096]{1,0:T(8,128)(2,1)}, bf16[256,4096]{1,0:T(8,128)(2,1)}, u32[]{:S(2)}, u32[]{:S(2)}) collective-permute-start(bf16[256,4096]{1,0:T(8,128)(2,1)} %add_convert_fusion), channel_id=1, source_target_pairs={{0,8},{4,12},{8,0},{12,4},{16,24},{20,28},{24,16},{28,20},{1,9},{5... | collective-permute-start | bytes 6291464 | tf_op jit(solution)/shard_map/ppermute | solution.py:19
  392.1 90.3 %collective-permute-start.56 = (bf16[64,2048]{1,0:T(8,128)(2,1)S(1)}, bf16[64,2048]{1,0:T(8,128)(2,1)S(1)}, u32[]{:S(2)}, u32[]{:S(2)}) collective-permute-start(bf16[64,2048]{1,0:T(8,128)(2,1)S(1)} %copy-done.74), channel_id=1, source_target_pairs={{0,3},{1,2},{2,1},{3,0},{4,7},{5,6},{6,5},{7,4},{8,11},{9,10},{10,... | collective-permute-start | bytes 786440 | tf_op jit(solution)/shard_map/ppermute | solution.py:19
  395.1 84.2 %collective-permute-start.61 = (bf16[512,512]{1,0:T(8,128)(2,1)S(1)}, bf16[512,512]{1,0:T(8,128)(2,1)S(1)}, u32[]{:S(2)}, u32[]{:S(2)}) collective-permute-start(bf16[512,512]{1,0:T(8,128)(2,1)S(1)} %add_convert_fusion.4), channel_id=1, source_target_pairs={{0,8},{4,12},{8,0},{12,4},{16,24},{20,28},{24,16},{28,20},{1,9},{5... | collective-permute-start | bytes 1572872 | tf_op jit(solution)/shard_map/ppermute | solution.py:19
  423.1 106.5 %collective-permute-start.72 = (bf16[256,2048]{1,0:T(8,128)(2,1)}, bf16[256,2048]{1,0:T(8,128)(2,1)}, u32[]{:S(2)}, u32[]{:S(2)}) collective-permute-start(bf16[256,2048]{1,0:T(8,128)(2,1)} %add_convert_fusion.2), channel_id=1, source_target_pairs={{0,8},{4,12},{8,0},{12,4},{16,24},{20,28},{24,16},{28,20},{1,9},{5... | collective-permute-start | bytes 3145736 | tf_op jit(solution)/shard_map/ppermute | solution.py:19
  479.3 54.8 %collective-permute-start.59 = (bf16[256,1536]{1,0:T(8,128)(2,1)}, bf16[256,1536]{1,0:T(8,128)(2,1)S(1)}, u32[]{:S(2)}, u32[]{:S(2)}) collective-permute-start(bf16[256,1536]{1,0:T(8,128)(2,1)} %add_convert_fusion.3), channel_id=1, source_target_pairs={{0,16},{4,20},{8,24},{12,28},{16,0},{20,4},{24,8},{28,12},{1,17},{... | collective-permute-start | bytes 2359304 | tf_op jit(solution)/shard_map/ppermute | solution.py:19
  479.8 46.8 %collective-permute-start.62 = (bf16[256,512]{1,0:T(8,128)(2,1)S(1)}, bf16[256,512]{1,0:T(8,128)(2,1)S(1)}, u32[]{:S(2)}, u32[]{:S(2)}) collective-permute-start(bf16[256,512]{1,0:T(8,128)(2,1)S(1)} %add_convert_fusion.5), channel_id=1, source_target_pairs={{0,16},{4,20},{8,24},{12,28},{16,0},{20,4},{24,8},{28,12},{1,17},{... | collective-permute-start | bytes 786440 | tf_op jit(solution)/shard_map/ppermute | solution.py:19
  (133 other events, 1629.8 us)
